TPU v7x, 128 devices: a whole 4x4x4 slice. The times are simulated.
128 devices in a mesh: sfc: 128 (over y, z, x, core).
Axes of the slice: x: 4, y: 4, z: 4, core: 2. Of those that a mesh axis runs over, the one named last changes fastest.
Arguments:
- state: float32 [5, 8192, 512], P(None, 'sfc'), may hold values from -0.47 to 4.3, as said below
- volume: int32 [8192, 512], P('sfc'), may hold values from 1 to 8, as said below
- neighbour: int32 [8192, 6], P('sfc'), may hold values from -1 to 8191, as said below
- parent: int32 [8192], P('sfc'), may hold values from 0 to 8191, as said below
Outputs:
- fine_state: float32 [5, 8192, 512], P(None, 'sfc')
- coarse_state: float32 [5, 1024, 512], P(None, 'sfc')
- coarse_residual: float32 [5, 1024, 512], P(None, 'sfc')
Inputs may be any that keep to these rules, and one draw needn't show every extreme that they name: `state`: each cell has density 0.65 to 1.55, x velocity 0.2 to 0.8, y and z velocity of size 0.3 at most, pressure 0.55 to 1.45, and total energy = pressure / 0.4 + half the density times the squared speed. `volume`: every cell of a brick that is not cut holds 8; a cut brick has some cell under 8. One device's 64 bricks hold at most 16 cut bricks, and some device holds exactly 16. `neighbour`: the fine bricks form a grid of 32 x 16 x 16, periodic along y, with -1 on the far-field faces at the ends of x and z. The grid is cut into cubes of 4 x 4 x 4 bricks, ordered along a Morton curve: device d holds the cube whose coordinates (in cubes) have bit i // 3 of x, y or z equal to bit i of d, as i % 3 is 0, 1 or 2, as bricks d * 64 to (d + 1) * 64 - 1 in no particular order. The relation is symmetric. `parent`: every pair of a coarse brick and an octant occurs exactly once; the octant gives the parities of the fine brick's x, y and z positions. The coarse level is the fine grid halved, ordered along its own Morton curve and cut into runs of 8 that start half a run later than the fine level's cuts: coarse brick c is held by device c // 8, and of each device's fine bricks exactly 32 have their parents on the next device (the last device's on device 0) and the rest on the device itself.
All inputs are finite; a program needn't handle non-finite values.
Results may differ from a plain program's by a relative error of at most 0.00002.
Values sent between devices are 32-bit elements; how exact they have to be, the bound alone decides.
No kernel may reach another device: no remote copies, remote signals or barrier semaphores. Data moves between devices by JAX's collectives and lax.ppermute only.
A program may use at most 128 MiB of HBM per device.

v0:
```python
import jax
import jax.numpy as jnp
from jax import lax
from jax.experimental import pallas as pl
from jax.experimental.pallas import tpu as pltpu
from jax.sharding import PartitionSpec as P


ROWS = 256
LANES = 128
AXIS = "sfc"
HEAT_RATIO = 1.4
CFL_NUMBER = 0.25
FIRST_SECTION = 0.5
STREAM = (1.0, 0.5, 0.0, 0.0, 1.0 / (HEAT_RATIO * (HEAT_RATIO - 1.0)) + 0.125)
F32 = jnp.float32
BF16 = jnp.bfloat16
I32 = jnp.int32


def bits_of(direction, count):
    return [bit for bit in range(count.bit_length() - 1) if bit % 3 == direction]


def coordinates(device, count):
    return [
        sum((device >> bit & 1) << place for place, bit in enumerate(bits_of(direction, count)))
        for direction in range(3)
    ]


def pair_swaps(count):
    extents = [1 << len(bits_of(direction, count)) for direction in range(3)]
    number = {tuple(coordinates(device, count)): device for device in range(count)}
    swaps = []
    for direction in range(3):
        for other in (0, 1):
            pairs = []
            for device in range(count):
                place = coordinates(device, count)
                step = 1 if place[direction] % 2 == other else -1
                place[direction] = (place[direction] + step) % extents[direction]
                pairs.append((device, number[tuple(place)]))
            swaps.append(pairs)
    return swaps


def cube_place(device_ref, count):
    device = device_ref[0]
    place = coordinates(device, count)
    even = [place[direction] % 2 == 0 for direction in range(3)]
    far = [None, None, None]
    for direction in (0, 2):
        last = (1 << len(bits_of(direction, count))) - 1
        far[direction] = jnp.logical_or(place[direction] == 0, place[direction] == last)
    return device, even, far


def lane_index(shape=(8, LANES)):
    return lax.broadcasted_iota(I32, shape, len(shape) - 1)


def row_index(shape=(8, LANES)):
    return lax.broadcasted_iota(I32, shape, 0)


def turn(x, shift, axis):
    extent = x.shape[axis]
    shift = shift % extent
    return x if shift == 0 else pltpu.roll(x, shift, axis)


def place_of_register(i, iy):
    return pl.ds((i * 8 + iy) * 8, 8)


def slots():
    lane = lane_index()
    return lane & 7, lane >> 5, lane >> 3 & 3


LANE_STEP = (1, 32, 8)
EDGE = (7, 3, 3)
PACK = (8, 4, 4)


def layer_register(ref, lead, direction, side, number):
    if direction == 0:
        return ref[lead + (place_of_register(3 * side, number), slice(None))]
    if direction == 1:
        return ref[lead + (place_of_register(number, 7 * side), slice(None))]
    return ref[lead + (pl.ds(number * 64 + 7 * side, 8, stride=8), slice(None))]


def packed_layer(ref, lead, direction, side, slot):
    step, edge = LANE_STEP[direction], EDGE[direction] * side
    result = None
    for number in range(PACK[direction]):
        piece = turn(
            layer_register(ref, lead, direction, side, number), (number - edge) * step, 1
        )
        result = piece if result is None else jnp.where(slot == number, piece, result)
    return result


def write_messages(refs, message_refs, even):
    slot = slots()
    for variable, (ref, lead) in enumerate(refs):
        for direction in range(3):
            low = packed_layer(ref, lead, direction, 0, slot[direction])
            high = packed_layer(ref, lead, direction, 1, slot[direction])
            message_refs[2 * direction][variable] = jnp.where(even[direction], high, low)
            message_refs[2 * direction + 1][variable] = jnp.where(even[direction], low, high)


def primitives(conserved):
    density, mx, my, mz, energy = conserved
    inverse = 1.0 / density
    u, v, w = mx * inverse, my * inverse, mz * inverse
    pressure = (HEAT_RATIO - 1.0) * (energy - 0.5 * (mx * u + my * v + mz * w))
    sound = jnp.sqrt(HEAT_RATIO * pressure * inverse)
    return u, v, w, pressure, sound


def face_terms(left, right, aperture, direction, with_speed=True):
    ul, vl, pl_, cl = left
    ur, vr, pr, cr = right
    speed = jnp.maximum(jnp.abs(vl) + cl, jnp.abs(vr) + cr)
    half = 0.5 * aperture
    sums = [ul[1 + direction] + ur[1 + direction]]
    for momentum in (1, 2, 3):
        term = ul[momentum] * vl + ur[momentum] * vr
        if momentum == 1 + direction:
            term = term + (pl_ + pr)
        sums.append(term)
    sums.append((ul[4] + pl_) * vl + (ur[4] + pr) * vr)
    terms = [half * (sums[q] - speed * (ur[q] - ul[q])) for q in range(5)]
    if with_speed:
        terms.append(aperture * speed)
    return terms


def interior_body(u_ref, frac_ref, res_ref, prim_ref, wx_ref, with_speed):
    count = 6 if with_speed else 5
    sign = [-1.0] * 5 + [1.0]
    rows = row_index()
    slot = slots()
    for register in range(32):
        at = pl.ds(register * 8, 8)
        for q, value in enumerate(primitives([u_ref[q, at, :] for q in range(5)])):
            prim_ref[q, at, :] = value

    def cell(at, direction):
        return (
            [u_ref[q, at, :] for q in range(5)],
            prim_ref[direction, at, :],
            prim_ref[3, at, :],
            prim_ref[4, at, :],
        )

    def turned(side, shift, axis):
        return ([turn(x, shift, axis) for x in side[0]],) + tuple(
            turn(x, shift, axis) for x in side[1:]
        )

    def less(total, terms):
        return [total[q] - terms[q] if q < 5 else total[q] + terms[q] for q in range(count)]

    def plus(total, terms):
        return [total[q] + terms[q] for q in range(count)]

    for i in range(4):
        wy = None
        for iy in range(8):
            at = place_of_register(i, iy)
            frac = frac_ref[at, :]
            here = cell(at, 2)
            wz = face_terms(
                here,
                turned(here, -1, 0),
                jnp.where(rows == 7, 0.0, jnp.minimum(frac, turn(frac, -1, 0))),
                2,
                with_speed,
            )
            total = less(wz, [turn(x, 1, 0) for x in wz])
            if wy is not None:
                total = less(total, wy)
            if iy < 7:
                up = place_of_register(i, iy + 1)
                wy = face_terms(
                    cell(at, 1), cell(up, 1), jnp.minimum(frac, frac_ref[up, :]), 1, with_speed
                )
                total = plus(total, wy)
            if i > 0:
                total = less(total, [wx_ref[q, pl.ds(iy * 8, 8), :] for q in range(count)])
            if i < 3:
                up = place_of_register(i + 1, iy)
                wx = face_terms(
                    cell(at, 0), cell(up, 0), jnp.minimum(frac, frac_ref[up, :]), 0, with_speed
                )
                for q in range(count):
                    wx_ref[q, pl.ds(iy * 8, 8), :] = wx[q]
                total = plus(total, wx)
            for q in range(count):
                res_ref[q, at, :] = total[q]

    for direction in range(3):
        step = LANE_STEP[direction]
        for number in range(PACK[direction]):
            if direction == 0:
                top, bottom = place_of_register(3, number), place_of_register(0, number)
            elif direction == 1:
                top, bottom = place_of_register(number, 7), place_of_register(number, 0)
            else:
                top = pl.ds(number * 64 + 7, 8, stride=8)
                bottom = pl.ds(number * 64, 8, stride=8)
            aperture = jnp.where(
                slot[direction] == EDGE[direction],
                0.0,
                jnp.minimum(frac_ref[top, :], turn(frac_ref[bottom, :], -step, 1)),
            )
            terms = face_terms(
                cell(top, direction),
                turned(cell(bottom, direction), -step, 1),
                aperture,
                direction,
                with_speed,
            )
            for q in range(count):
                res_ref[q, top, :] = res_ref[q, top, :] + terms[q]
                back = turn(terms[q], step, 1)
                res_ref[q, bottom, :] = res_ref[q, bottom, :] + sign[q] * back


def boundary_body(
    res_ref, aperture_of, own_refs, ghost_refs, even, far, with_speed
):
    count = 6 if with_speed else 5
    slot = slots()
    for direction in range(3):
        terms = []
        for other in (0, 1):
            own_ref, ghost_ref = own_refs[2 * direction + other], ghost_refs[2 * direction + other]
            own = [own_ref[q] for q in range(5)]
            ghost = [ghost_ref[q] for q in range(5)]
            if other == 1 and far[direction] is not None:
                ghost = [jnp.where(far[direction], STREAM[q], ghost[q]) for q in range(5)]
            own_is_left = even[direction] if other == 0 else jnp.logical_not(even[direction])
            left = [jnp.where(own_is_left, own[q], ghost[q]) for q in range(5)]
            right = [jnp.where(own_is_left, ghost[q], own[q]) for q in range(5)]
            sides = []
            for values in (left, right):
                prims = primitives(values)
                sides.append((values, prims[direction], prims[3], prims[4]))
            terms.append(
                face_terms(sides[0], sides[1], aperture_of(direction, other), direction, with_speed)
            )
        step = LANE_STEP[direction]
        for q in range(count):
            high = jnp.where(even[direction], terms[0][q], terms[1][q])
            low = jnp.where(even[direction], terms[1][q], terms[0][q])
            for side, value in ((1, high), (0, low)):
                edge = EDGE[direction] * side
                for number in range(PACK[direction]):
                    if direction == 0:
                        at = place_of_register(3 * side, number)
                    elif direction == 1:
                        at = place_of_register(number, 7 * side)
                    else:
                        at = pl.ds(number * 64 + 7 * side, 8, stride=8)
                    piece = jnp.where(
                        slot[direction] == edge, turn(value, (edge - number) * step, 1), 0.0
                    )
                    if side == 0 and q < 5:
                        piece = -piece
                    res_ref[q, at, :] = res_ref[q, at, :] + piece


def box_sum(registers):
    rows = row_index()
    xs = slots()[0]
    result = []
    for i in range(4):
        along_z = [
            x
            + jnp.where(rows == 0, 0.0, turn(x, 1, 0))
            + jnp.where(rows == 7, 0.0, turn(x, -1, 0))
            for x in registers[i]
        ]
        along_y = []
        for iy in range(8):
            value = along_z[iy]
            if iy > 0:
                value = value + along_z[iy - 1]
            if iy < 7:
                value = value + along_z[iy + 1]
            along_y.append(value)
        result.append(along_y)
    boxed = [[None] * 8 for _ in range(4)]
    for iy in range(8):
        before = jnp.where(xs & 1 == 1, turn(result[3][iy], 1, 1), 0.0)
        after = jnp.where(xs & 1 == 0, turn(result[0][iy], -1, 1), 0.0)
        line = [before] + [result[i][iy] for i in range(4)] + [after]
        for i in range(4):
            boxed[i][iy] = line[i] + line[i + 1] + line[i + 2]
    return boxed


def split3(x):
    high = x.astype(BF16)
    rest = x - high.astype(F32)
    middle = rest.astype(BF16)
    low = (rest - middle.astype(F32)).astype(BF16)
    return high, middle, low


def as_column(row, count):
    same = row_index((count, count)) == lane_index((count, count))
    return jnp.sum(jnp.where(same, row, 0), axis=1, keepdims=True)


def brick_lane(device, neighbour_ref, parent_column):
    outside = (neighbour_ref[...] >> 6) != device
    outside = outside.astype(I32)
    place = []
    for direction in range(3):
        odd = parent_column >> (2 - direction) & 1
        upper = jnp.where(
            odd == 1,
            outside[:, 2 * direction + 1 : 2 * direction + 2],
            1 - outside[:, 2 * direction : 2 * direction + 1],
        )
        place.append(odd + 2 * upper)
    return place[1] * 32 + place[2] * 8 + place[0] * 2


def prepare_kernel(count, device_ref, state_ref, volume_ref, neighbour_ref, parent_ref, *outs):
    u_ref, frac_ref = outs[0:2]
    message_refs = outs[2:8]
    device, even, _ = cube_place(device_ref, count)
    lane = brick_lane(device, neighbour_ref, as_column(parent_ref[...], 64))
    spread = [
        (lane_index((64, LANES)) == lane + half).astype(F32).astype(BF16) for half in (0, 1)
    ]
    tripled = [jnp.concatenate([s, s, s], axis=0) for s in spread]
    dims = (((0,), (0,)), ((), ()))
    for q in range(5):
        parts = jnp.concatenate(split3(state_ref[q]), axis=0)
        u_ref[q] = lax.dot_general(
            parts[:, 0:256], tripled[0], dims, preferred_element_type=F32
        ) + lax.dot_general(parts[:, 256:512], tripled[1], dims, preferred_element_type=F32)
    volume = (volume_ref[...].astype(F32) / 8.0).astype(BF16)
    frac_ref[...] = lax.dot_general(
        volume[:, 0:256], spread[0], dims, preferred_element_type=F32
    ) + lax.dot_general(volume[:, 256:512], spread[1], dims, preferred_element_type=F32)
    write_messages([(u_ref, (q,)) for q in range(5)] + [(frac_ref, ())], message_refs, even)


def tables_kernel(count, device_ref, neighbour_ref, parent_ref, spread_ref, order_ref, pick_ref):
    device = device_ref[0]
    parent_row = parent_ref[...]
    parent_column = as_column(parent_row, 64)
    lane = brick_lane(device, neighbour_ref, parent_column)
    lanes = lane_index((64, LANES))
    spread = [(lanes == lane + half).astype(F32) for half in (0, 1)]
    spread_ref[0] = spread[0]
    spread_ref[1] = spread[1]
    slot = parent_column >> 3 & 7
    kept = (parent_column >> 6 == device).astype(I32)
    rank = []
    present_kept = None
    for flag in (kept, 1 - kept):
        present = jnp.max(
            jnp.where(lanes == slot, flag, 0), axis=0, keepdims=True
        )
        if present_kept is None:
            present_kept = present
        rank.append(jnp.sum(jnp.where(lanes < slot, present, 0), axis=1, keepdims=True))
    key = jnp.where(kept == 1, rank[0], 4 + rank[1]).astype(F32)
    key_row = jnp.sum((spread[0] + spread[1]) * key, axis=0, keepdims=True).astype(I32)
    lane_row = lane_index((1, LANES))
    half, lx, lz, ly = lane_row & 1, lane_row >> 1 & 3, lane_row >> 3 & 3, lane_row >> 5
    part = ((lx & 1) * 2 + half) * 4 + (ly & 1) * 2 + (lz & 1)
    order_ref[...] = (row_index((LANES, LANES)) == part * 8 + key_row).astype(F32)
    slots8, lanes8 = row_index(), lane_index()
    mine = jnp.sum(jnp.where(lanes8 == slots8, present_kept, 0), axis=1, keepdims=True)
    before = jnp.sum(jnp.where(lanes8 < slots8, present_kept, 0), axis=1, keepdims=True)
    source = jnp.where(mine == 1, before, 4 + slots8 - before)
    pick_ref[...] = (source == lanes8).astype(F32)


def mixing_kernel(frac_ref, mix_ref):
    frac = [[frac_ref[place_of_register(i, iy), :] for iy in range(8)] for i in range(4)]
    boxed = box_sum(frac)
    for i in range(4):
        for iy in range(8):
            mix_ref[place_of_register(i, iy), :] = (1.0 - frac[i][iy]) / boxed[i][iy]


def interior_kernel(with_speed, u_ref, frac_ref, res_ref, prim_ref, wx_ref):
    interior_body(u_ref, frac_ref, res_ref, prim_ref, wx_ref, with_speed)


def update_kernel(count, first, device_ref, *refs):
    base_ref, frac_ref, mix_ref, inner_ref = refs[0:4]
    own_refs, ghost_refs = refs[4:10], refs[10:16]
    refs = refs[16:]
    if first:
        new_ref, message_refs, faces_ref, res_ref = refs[0], refs[1:7], refs[7], refs[8]
    else:
        faces_ref, new_ref, message_refs, res_ref = refs[0], refs[1], refs[2:8], refs[8]
    _, even, far = cube_place(device_ref, count)
    res_ref[...] = inner_ref[...]

    def aperture_of(direction, other):
        number = 2 * direction + other
        if not first:
            return faces_ref[number]
        own, ghost = own_refs[number][5], ghost_refs[number][5]
        if other == 1 and far[direction] is not None:
            ghost = jnp.where(far[direction], own, ghost)
        aperture = jnp.minimum(own, ghost)
        faces_ref[number] = aperture
        return aperture

    boundary_body(res_ref, aperture_of, own_refs, ghost_refs, even, far, True)
    for register in range(32):
        at = pl.ds(register * 8, 8)
        scale = frac_ref[at, :] * (-CFL_NUMBER / res_ref[5, at, :])
        for q in range(5):
            res_ref[q, at, :] = res_ref[q, at, :] * scale
    factor = FIRST_SECTION if first else 1.0
    for q in range(5):
        share = [[res_ref[q, place_of_register(i, iy), :] for iy in range(8)] for i in range(4)]
        boxed = box_sum(share)
        for i in range(4):
            for iy in range(8):
                at = place_of_register(i, iy)
                mixed = share[i][iy] + mix_ref[at, :] * boxed[i][iy]
                if first:
                    mixed = factor * mixed
                new_ref[q, at, :] = base_ref[q, at, :] + mixed
    write_messages([(new_ref, (q,)) for q in range(5)], message_refs, even)


def coarse_rows(registers, order3, rows_ref, half_ref):
    for i in (0, 1):
        for jy in range(4):
            half_ref[pl.ds((i * 4 + jy) * 8, 8), :] = (
                registers(2 * i, 2 * jy)
                + registers(2 * i, 2 * jy + 1)
                + registers(2 * i + 1, 2 * jy)
                + registers(2 * i + 1, 2 * jy + 1)
            )
    for i in (0, 1):
        for jy in range(4):
            start = (i * 4 + jy) * 8
            rows_ref[pl.ds(i * 64 + jy * 8, 4), :] = (
                half_ref[pl.ds(start, 4, stride=2), :] + half_ref[pl.ds(start + 1, 4, stride=2), :]
            )
    parts = jnp.concatenate(split3(rows_ref[...]), axis=1)
    placed = lax.dot_general(order3, parts, (((1,), (1,)), ((), ())), preferred_element_type=F32)
    tiles = []
    for tile in range(4):
        total = None
        for number in range(4):
            start = (tile * 4 + number) * 8
            piece = turn(placed[start : start + 8, :], (number // 2) * 32 + (number % 2) * 4, 1)
            total = piece if total is None else total + piece
        tiles.append(total)
    return jnp.concatenate(tiles, axis=1)


def tripled_order(order_ref):
    order = order_ref[...].astype(BF16)
    return jnp.concatenate([order, order, order], axis=1)


def state_kernel(u_ref, frac_ref, spread_ref, order_ref, out_ref, kept_ref, sent_ref, rows_ref, half_ref):
    rows_ref[...] = jnp.zeros_like(rows_ref)
    tripled = []
    for half in (0, 1):
        spread = spread_ref[half].astype(BF16)
        tripled.append(jnp.concatenate([spread, spread, spread], axis=1))
    order3 = tripled_order(order_ref)
    dims = (((1,), (1,)), ((), ()))
    for q in range(5):
        parts = jnp.concatenate(split3(u_ref[q]), axis=1)
        for half in (0, 1):
            out_ref[q, :, pl.ds(half * 256, 256)] = lax.dot_general(
                tripled[half], parts, dims, preferred_element_type=F32
            )
    for q in range(6):
        if q < 5:
            def registers(i, iy, q=q):
                at = place_of_register(i, iy)
                return frac_ref[at, :] * u_ref[q, at, :]
        else:
            def registers(i, iy):
                return frac_ref[place_of_register(i, iy), :]
        sums = coarse_rows(registers, order3, rows_ref, half_ref)
        kept_ref[q] = sums[0:4]
        sent_ref[q] = sums[4:8]


def residual_kernel(count, device_ref, *refs):
    inner_ref, faces_ref, order_ref = refs[0:3]
    own_refs, ghost_refs = refs[3:9], refs[9:15]
    kept_ref, sent_ref, res_ref, rows_ref, half_ref = refs[15:20]
    _, even, far = cube_place(device_ref, count)
    res_ref[...] = inner_ref[...]
    boundary_body(
        res_ref,
        lambda direction, other: faces_ref[2 * direction + other],
        own_refs,
        ghost_refs,
        even,
        far,
        False,
    )
    rows_ref[...] = jnp.zeros_like(rows_ref)
    order3 = tripled_order(order_ref)
    for q in range(5):
        sums = coarse_rows(
            lambda i, iy: res_ref[q, place_of_register(i, iy), :], order3, rows_ref, half_ref
        )
        kept_ref[q] = sums[0:4]
        sent_ref[q] = sums[4:8]


def coarse_kernel(pick_ref, kept_state_ref, kept_res_ref, state_ref, res_ref, out_state_ref, out_res_ref):
    pick = pick_ref[...]

    def choose(kept, received):
        result = None
        for source in range(8):
            row = kept[source : source + 1] if source < 4 else received[source - 4 : source - 3]
            piece = jnp.where(pick[:, source : source + 1] > 0.5, row, 0.0)
            result = piece if result is None else result + piece
        return result

    weight = choose(kept_state_ref[5], state_ref[5])
    for q in range(5):
        out_state_ref[q] = choose(kept_state_ref[q], state_ref[q]) / weight
        out_res_ref[q] = choose(kept_res_ref[q], res_ref[q])


def f32(*shape):
    return jax.ShapeDtypeStruct(shape, F32)


def call(kernel, outs, scratch, args, name, smem=1):
    vmem = pl.BlockSpec(memory_space=pltpu.VMEM)
    specs = [pl.BlockSpec(memory_space=pltpu.SMEM)] * smem + [vmem] * (len(args) - smem)
    return pl.pallas_call(
        kernel,
        out_shape=outs,
        in_specs=specs,
        out_specs=[vmem] * len(outs),
        scratch_shapes=[pltpu.VMEM(shape, F32) for shape in scratch],
        name=name,
        cost_estimate=pl.CostEstimate(flops=8_000_000, bytes_accessed=4_000_000, transcendentals=0),
    )(*args)


def solution(mesh):
    count = mesh.shape[AXIS]
    swaps = pair_swaps(count)
    forward = [(device, (device + 1) % count) for device in range(count)]

    def exchange(messages):
        ghosts = [None] * 6
        for number in (5, 3, 1, 4, 2, 0):
            ghosts[number] = lax.ppermute(messages[number], AXIS, swaps[number])
        return ghosts

    def interior(u, frac, with_speed, name):
        rows = 6 if with_speed else 5
        return call(
            lambda *refs: interior_kernel(with_speed, *refs),
            [f32(rows, ROWS, LANES)],
            [(5, ROWS, LANES), (rows, 64, LANES)],
            [u, frac],
            name,
            0,
        )[0]

    def local(state, volume, neighbour, parent):
        device = lax.axis_index(AXIS).astype(I32).reshape(1)
        parent = parent.reshape(1, 64)
        grid = f32(5, ROWS, LANES)
        u, frac, *sent = call(
            lambda *refs: prepare_kernel(count, *refs),
            [grid, f32(ROWS, LANES)] + [f32(6, 8, LANES)] * 6,
            [],
            [device, state, volume, neighbour, parent],
            "prepare",
        )
        ghosts = exchange(sent)
        spread, order, pick = call(
            lambda *refs: tables_kernel(count, *refs),
            [f32(2, 64, LANES), f32(LANES, LANES), f32(8, LANES)],
            [],
            [device, neighbour, parent],
            "tables",
        )
        mix = call(mixing_kernel, [f32(ROWS, LANES)], [], [frac], "mixing", 0)[0]
        inner = interior(u, frac, True, "interior_1")
        middle, *rest = call(
            lambda *refs: update_kernel(count, True, *refs),
            [grid] + [f32(5, 8, LANES)] * 6 + [f32(6, 8, LANES)],
            [(6, ROWS, LANES)],
            [device, u, frac, mix, inner, *sent, *ghosts],
            "update_1",
        )
        sent, faces = rest[0:6], rest[6]
        ghosts = exchange(sent)
        inner = interior(middle, frac, True, "interior_2")
        fine, *sent = call(
            lambda *refs: update_kernel(count, False, *refs),
            [grid] + [f32(5, 8, LANES)] * 6,
            [(6, ROWS, LANES)],
            [device, u, frac, mix, inner, *sent, *ghosts, faces],
            "update_2",
        )
        ghosts = exchange(sent)
        inner = interior(fine, frac, False, "interior_3")
        fine_out, kept_state, sent_state = call(
            state_kernel,
            [f32(5, 64, 512), f32(6, 4, 512), f32(6, 4, 512)],
            [(LANES, LANES), (64, LANES)],
            [fine, frac, spread, order],
            "restrict_state",
            0,
        )
        kept_res, sent_res = call(
            lambda *refs: residual_kernel(count, *refs),
            [f32(5, 4, 512), f32(5, 4, 512)],
            [(5, ROWS, LANES), (LANES, LANES), (64, LANES)],
            [device, inner, faces, order, *sent, *ghosts],
            "restrict_residual",
        )
        got_state = lax.ppermute(sent_state, AXIS, forward)
        got_res = lax.ppermute(sent_res, AXIS, forward)
        coarse_state, coarse_residual = call(
            coarse_kernel,
            [f32(5, 8, 512), f32(5, 8, 512)],
            [],
            [pick, kept_state, kept_res, got_state, got_res],
            "coarse",
            0,
        )
        return fine_out, coarse_state, coarse_residual

    in_specs = (P(None, AXIS, None), P(AXIS, None), P(AXIS, None), P(AXIS))
    out_specs = (P(None, AXIS, None), P(None, AXIS, None), P(None, AXIS, None))
    return jax.shard_map(local, mesh=mesh, in_specs=in_specs, out_specs=out_specs, check_vma=False)
```

profile of v0, /device:TPU:0, one launch (start us, length us, event | category | flops | bytes accessed | tf_op | source)
XLA Modules:
  0.0 76.9 jit_solution(2932387435846551085)
XLA Ops:
  0.6 0.7 copy-done.20
  1.3 0.7 copy.7.refs_3_.refs_1_
  2.0 2.9 %prepare.1 = (f32[5,256,128]{2,1,0:T(8,128)}, f32[256,128]{1,0:T(8,128)}, f32[6,8,128]{2,1,0:T(8,128)}, f32[6,8,128]{2,1,0:T(8,128)}, f32[6,8,128]{2,1,0:T(8,128...) custom-call(s32[1]{0:T(128)} %bitcast.refs_0_, f32[5,64,512]{2,1,0:T(8,128)} %refs_1_.2, ...), custom_call_target="tpu_custom_call" | custom-call | flops 8000000 | bytes 4000000 | tf_op jit(solution)/shard_map/prepare/pallas_call | solution.py:555
  5.0 4.8 %collective-permute-start.1 = (f32[6,8,128]{2,1,0:T(8,128)}, f32[6,8,128]{2,1,0:T(8,128)S(1)}, u32[]{:S(2)}, u32[]{:S(2)}) collective-permute-start(f32[6,8,128]{2,1,0:T(8,128)} %get-tuple-element.39.refs_6_), channel_id=1, source_target_pairs={{0,73},{1,8},{2,75},{3,10},{4,77},{5,12},{6,79},{7,14},{8,1},{9,64... | collective-permute-start | bytes 73736 | tf_op jit(solution)/shard_map/ppermute | solution.py:574
  9.7 1.5 %collective-permute-start.2 = (f32[6,8,128]{2,1,0:T(8,128)}, f32[6,8,128]{2,1,0:T(8,128)S(1)}, u32[]{:S(2)}, u32[]{:S(2)}) collective-permute-start(f32[6,8,128]{2,1,0:T(8,128)} %get-tuple-element.40.refs_7_), channel_id=1, source_target_pairs={{0,2},{1,3},{2,0},{3,1},{4,6},{5,7},{6,4},{7,5},{8,10},{9,11},{10,... | collective-permute-start | bytes 73736 | tf_op jit(solution)/shard_map/ppermute | solution.py:574
  11.2 3.6 %collective-permute-start.3 = (f32[6,8,128]{2,1,0:T(8,128)}, f32[6,8,128]{2,1,0:T(8,128)S(1)}, u32[]{:S(2)}, u32[]{:S(2)}) collective-permute-start(f32[6,8,128]{2,1,0:T(8,128)} %get-tuple-element.41.refs_8_), channel_id=1, source_target_pairs={{0,18},{1,19},{2,16},{3,17},{4,22},{5,23},{6,20},{7,21},{8,26},{9,... | collective-permute-start | bytes 73736 | tf_op jit(solution)/shard_map/ppermute | solution.py:574
  14.8 3.0 %collective-permute-start.4 = (f32[6,8,128]{2,1,0:T(8,128)}, f32[6,8,128]{2,1,0:T(8,128)S(1)}, u32[]{:S(2)}, u32[]{:S(2)}) collective-permute-start(f32[6,8,128]{2,1,0:T(8,128)} %get-tuple-element.42.refs_9_), channel_id=1, source_target_pairs={{0,4},{1,5},{2,6},{3,7},{4,0},{5,1},{6,2},{7,3},{8,12},{9,13},{10,... | collective-permute-start | bytes 73736 | tf_op jit(solution)/shard_map/ppermute | solution.py:574
  17.8 0.6 collective-permute-start.5
  18.4 1.6 %mixing.1.refs_3_ = f32[256,128]{1,0:T(8,128)} custom-call(f32[256,128]{1,0:T(8,128)} %get-tuple-element.37.frac_ref.refs_1_.refs_2_), custom_call_target="tpu_custom_call" | custom-call | flops 8000000 | bytes 4000000 | tf_op jit(solution)/shard_map/mixing/pallas_call | solution.py:555
  20.1 3.3 %interior_1.1.refs_4_ = f32[6,256,128]{2,1,0:T(8,128)} custom-call(f32[5,256,128]{2,1,0:T(8,128)} %get-tuple-element.36.refs_0_.refs_1_, f32[256,128]{1,0:T(8,128)} %get-tuple-element.37.frac_ref.refs_1_.refs_2_), custom_call_target="tpu_custom_call" | custom-call | flops 8000000 | bytes 4000000 | tf_op jit(solution)/shard_map/interior_1/pallas_call | solution.py:555
  23.4 0.8 %collective-permute-done.5.refs_16_ = f32[6,8,128]{2,1,0:T(8,128)S(1)} collective-permute-done((f32[6,8,128]{2,1,0:T(8,128)}, f32[6,8,128]{2,1,0:T(8,128)S(1)}, u32[]{:S(2)}, u32[]{:S(2)}) %collective-permute-start.5) | collective-permute-done | bytes 24608 | tf_op jit(solution)/shard_map/ppermute | solution.py:574
  24.9 3.2 %update_1.1 = (f32[5,256,128]{2,1,0:T(8,128)}, f32[5,8,128]{2,1,0:T(8,128)}, f32[5,8,128]{2,1,0:T(8,128)}, f32[5,8,128]{2,1,0:T(8,128)}, f32[5,8,128]{2,1,0:T(8,...) custom-call(s32[1]{0:T(128)} %bitcast.refs_0_, ...), custom_call_target="tpu_custom_call" | custom-call | flops 8000000 | bytes 4000000 | tf_op jit(solution)/shard_map/update_1/pallas_call | solution.py:555
  28.0 2.9 %collective-permute-start.10 = (f32[5,8,128]{2,1,0:T(8,128)}, f32[5,8,128]{2,1,0:T(8,128)S(1)}, u32[]{:S(2)}, u32[]{:S(2)}) collective-permute-start(f32[5,8,128]{2,1,0:T(8,128)} %get-tuple-element.49.refs_9_), channel_id=1, source_target_pairs={{0,4},{1,5},{2,6},{3,7},{4,0},{5,1},{6,2},{7,3},{8,12},{9,13},{10,... | collective-permute-start | bytes 61448 | tf_op jit(solution)/shard_map/ppermute | solution.py:574
  30.9 1.3 %collective-permute-start.11 = (f32[5,8,128]{2,1,0:T(8,128)}, f32[5,8,128]{2,1,0:T(8,128)S(1)}, u32[]{:S(2)}, u32[]{:S(2)}) collective-permute-start(f32[5,8,128]{2,1,0:T(8,128)} %get-tuple-element.50.refs_10_), channel_id=1, source_target_pairs={{0,36},{1,37},{2,38},{3,39},{4,32},{5,33},{6,34},{7,35},{8,44},{9,... | collective-permute-start | bytes 61448 | tf_op jit(solution)/shard_map/ppermute | solution.py:574
  32.3 1.4 %collective-permute-start.8 = (f32[5,8,128]{2,1,0:T(8,128)}, f32[5,8,128]{2,1,0:T(8,128)S(1)}, u32[]{:S(2)}, u32[]{:S(2)}) collective-permute-start(f32[5,8,128]{2,1,0:T(8,128)} %get-tuple-element.47.refs_7_), channel_id=1, source_target_pairs={{0,2},{1,3},{2,0},{3,1},{4,6},{5,7},{6,4},{7,5},{8,10},{9,11},{10,... | collective-permute-start | bytes 61448 | tf_op jit(solution)/shard_map/ppermute | solution.py:574
  33.7 0.9 %collective-permute-start.9 = (f32[5,8,128]{2,1,0:T(8,128)}, f32[5,8,128]{2,1,0:T(8,128)S(1)}, u32[]{:S(2)}, u32[]{:S(2)}) collective-permute-start(f32[5,8,128]{2,1,0:T(8,128)} %get-tuple-element.48.refs_8_), channel_id=1, source_target_pairs={{0,18},{1,19},{2,16},{3,17},{4,22},{5,23},{6,20},{7,21},{8,26},{9,... | collective-permute-start | bytes 61448 | tf_op jit(solution)/shard_map/ppermute | solution.py:574
  34.6 3.3 %interior_2.1.refs_4_ = f32[6,256,128]{2,1,0:T(8,128)} custom-call(f32[5,256,128]{2,1,0:T(8,128)} %get-tuple-element.44.refs_0_, f32[256,128]{1,0:T(8,128)} %get-tuple-element.37.frac_ref.refs_1_.refs_2_), custom_call_target="tpu_custom_call" | custom-call | flops 8000000 | bytes 4000000 | tf_op jit(solution)/shard_map/interior_2/pallas_call | solution.py:555
  38.2 1.9 %collective-permute-done.9.refs_14_ = f32[5,8,128]{2,1,0:T(8,128)S(1)} collective-permute-done((f32[5,8,128]{2,1,0:T(8,128)}, f32[5,8,128]{2,1,0:T(8,128)S(1)}, u32[]{:S(2)}, u32[]{:S(2)}) %collective-permute-start.9) | collective-permute-done | bytes 20512 | tf_op jit(solution)/shard_map/ppermute | solution.py:574
  40.7 3.1 %update_2.1 = (f32[5,256,128]{2,1,0:T(8,128)}, f32[5,8,128]{2,1,0:T(8,128)}, f32[5,8,128]{2,1,0:T(8,128)}, f32[5,8,128]{2,1,0:T(8,128)}, f32[5,8,128]{2,1,0:T(8,...) custom-call(s32[1]{0:T(128)} %bitcast.refs_0_, f32[5,256,128]{2,1,0:T(8,128)} %get-tuple-element.36.refs_0_.refs_1_, ...), custom_call_target="tpu_custom_call" | custom-call | flops 8000000 | bytes 4000000 | tf_op jit(solution)/shard_map/update_2/pallas_call | solution.py:555
  43.9 2.8 %collective-permute-start.13 = (f32[5,8,128]{2,1,0:T(8,128)}, f32[5,8,128]{2,1,0:T(8,128)S(1)}, u32[]{:S(2)}, u32[]{:S(2)}) collective-permute-start(f32[5,8,128]{2,1,0:T(8,128)} %get-tuple-element.59.refs_5_), channel_id=1, source_target_pairs={{0,73},{1,8},{2,75},{3,10},{4,77},{5,12},{6,79},{7,14},{8,1},{9,64... | collective-permute-start | bytes 61448 | tf_op jit(solution)/shard_map/ppermute | solution.py:574
  46.7 0.8 %collective-permute-start.14 = (f32[5,8,128]{2,1,0:T(8,128)}, f32[5,8,128]{2,1,0:T(8,128)S(1)}, u32[]{:S(2)}, u32[]{:S(2)}) collective-permute-start(f32[5,8,128]{2,1,0:T(8,128)} %get-tuple-element.60.refs_6_), channel_id=1, source_target_pairs={{0,2},{1,3},{2,0},{3,1},{4,6},{5,7},{6,4},{7,5},{8,10},{9,11},{10,... | collective-permute-start | bytes 61448 | tf_op jit(solution)/shard_map/ppermute | solution.py:574
  47.5 2.6 %collective-permute-start.15 = (f32[5,8,128]{2,1,0:T(8,128)}, f32[5,8,128]{2,1,0:T(8,128)S(1)}, u32[]{:S(2)}, u32[]{:S(2)}) collective-permute-start(f32[5,8,128]{2,1,0:T(8,128)} %get-tuple-element.61.refs_7_), channel_id=1, source_target_pairs={{0,18},{1,19},{2,16},{3,17},{4,22},{5,23},{6,20},{7,21},{8,26},{9,... | collective-permute-start | bytes 61448 | tf_op jit(solution)/shard_map/ppermute | solution.py:574
  50.1 3.0 %collective-permute-start.16 = (f32[5,8,128]{2,1,0:T(8,128)}, f32[5,8,128]{2,1,0:T(8,128)S(1)}, u32[]{:S(2)}, u32[]{:S(2)}) collective-permute-start(f32[5,8,128]{2,1,0:T(8,128)} %get-tuple-element.62.refs_8_), channel_id=1, source_target_pairs={{0,4},{1,5},{2,6},{3,7},{4,0},{5,1},{6,2},{7,3},{8,12},{9,13},{10,... | collective-permute-start | bytes 61448 | tf_op jit(solution)/shard_map/ppermute | solution.py:574
  53.1 0.9 %collective-permute-start.17 = (f32[5,8,128]{2,1,0:T(8,128)}, f32[5,8,128]{2,1,0:T(8,128)S(1)}, u32[]{:S(2)}, u32[]{:S(2)}) collective-permute-start(f32[5,8,128]{2,1,0:T(8,128)} %get-tuple-element.63.refs_9_), channel_id=1, source_target_pairs={{0,36},{1,37},{2,38},{3,39},{4,32},{5,33},{6,34},{7,35},{8,44},{9,... | collective-permute-start | bytes 61448 | tf_op jit(solution)/shard_map/ppermute | solution.py:574
  54.0 1.7 %tables.1 = (f32[2,64,128]{2,1,0:T(8,128)}, f32[128,128]{1,0:T(8,128)}, f32[8,128]{1,0:T(8,128)}) custom-call(s32[1]{0:T(128)} %bitcast.refs_0_, s32[64,6]{1,0:T(8,128)} %copy.7.refs_3_.refs_1_, s32[1,64]{1,0:T(1,128)} %bitcast.3), custom_call_target="tpu_custom_call" | custom-call | flops 8000000 | bytes 4000000 | tf_op jit(solution)/shard_map/tables/pallas_call | solution.py:555
  55.7 2.9 %restrict_state.1 = (f32[5,64,512]{2,1,0:T(8,128)}, f32[6,4,512]{2,1,0:T(4,128)}, f32[6,4,512]{2,1,0:T(4,128)}) custom-call(f32[5,256,128]{2,1,0:T(8,128)} %get-tuple-element.52.u_ref.refs_0_, f32[256,128]{1,0:T(8,128)} %get-tuple-element.37.frac_ref.refs_1_.refs_2_, f32[2,64,128]{2,1,0:T(8,128)} %get-tuple-element.53.spread_ref, ...), custom_call_target="tpu_custom_call" | custom-call | flops 8000000 | bytes 4000000 | tf_op jit(solution)/shard_map/restrict_state/pallas_call | solution.py:555
  58.7 3.1 %interior_3.1.refs_1_ = f32[5,256,128]{2,1,0:T(8,128)} custom-call(f32[5,256,128]{2,1,0:T(8,128)} %get-tuple-element.52.u_ref.refs_0_, f32[256,128]{1,0:T(8,128)} %get-tuple-element.37.frac_ref.refs_1_.refs_2_), custom_call_target="tpu_custom_call" | custom-call | flops 8000000 | bytes 4000000 | tf_op jit(solution)/shard_map/interior_3/pallas_call | solution.py:555
  63.0 2.5 %restrict_residual.1 = (f32[5,4,512]{2,1,0:T(4,128)}, f32[5,4,512]{2,1,0:T(4,128)}) custom-call(s32[1]{0:T(128)} %bitcast.refs_0_, f32[5,256,128]{2,1,0:T(8,128)} %interior_3.1.refs_1_, f32[6,8,128]{2,1,0:T(8,128)} %get-tuple-element.51.refs_17_.refs_2_, f32[128,128]{1,0:T(8,128)} %get-tuple-element.54.order_ref.refs_3_, ...), custom_call_target="tpu_custom_call" | custom-call | flops 8000000 | bytes 4000000 | tf_op jit(solution)/shard_map/restrict_residual/pallas_call | solution.py:555
  65.5 1.4 %collective-permute-start.19 = (f32[5,4,512]{2,1,0:T(4,128)}, f32[5,4,512]{2,1,0:T(4,128)S(1)}, u32[]{:S(2)}, u32[]{:S(2)}) collective-permute-start(f32[5,4,512]{2,1,0:T(4,128)} %get-tuple-element.66), channel_id=1, source_target_pairs={{0,1},{1,2},{2,3},{3,4},{4,5},{5,6},{6,7},{7,8},{8,9},{9,10},{10,1... | collective-permute-start | bytes 122888 | tf_op jit(solution)/shard_map/ppermute | solution.py:644
  66.9 0.9 %collective-permute-done.18.state_ref = f32[6,4,512]{2,1,0:T(4,128)S(1)} collective-permute-done((f32[6,4,512]{2,1,0:T(4,128)}, f32[6,4,512]{2,1,0:T(4,128)S(1)}, u32[]{:S(2)}, u32[]{:S(2)}) %collective-permute-start.18) | collective-permute-done | bytes 49184 | tf_op jit(solution)/shard_map/ppermute | solution.py:643
  67.8 6.8 %collective-permute-done.19.res_ref = f32[5,4,512]{2,1,0:T(4,128)S(1)} collective-permute-done((f32[5,4,512]{2,1,0:T(4,128)}, f32[5,4,512]{2,1,0:T(4,128)S(1)}, u32[]{:S(2)}, u32[]{:S(2)}) %collective-permute-start.19) | collective-permute-done | bytes 40992 | tf_op jit(solution)/shard_map/ppermute | solution.py:644
  75.2 1.6 %coarse.1 = (f32[5,8,512]{2,1,0:T(8,128)}, f32[5,8,512]{2,1,0:T(8,128)}) custom-call(f32[8,128]{1,0:T(8,128)} %get-tuple-element.56.pick_ref, f32[6,4,512]{2,1,0:T(4,128)} %get-tuple-element.57.kept_state_ref, f32[5,4,512]{2,1,0:T(4,128)} %get-tuple-element.64.kept_res_ref, f32[6,4,512]{2,1,0:T(4,128)} %copy-done, f32[5,4,512]{2,1,0:T(4,128)} %copy-done.1), custom_call_target="tpu_custom_call" | custom-call | flops 8000000 | bytes 4000000 | tf_op jit(solution)/shard_map/coarse/pallas_call | solution.py:555
  (62 shorter events, 3.5 us)
Async XLA Ops:
  4.9 12.9 %collective-permute-start = (f32[6,8,128]{2,1,0:T(8,128)}, f32[6,8,128]{2,1,0:T(8,128)S(1)}, u32[]{:S(2)}, u32[]{:S(2)}) collective-permute-start(f32[6,8,128]{2,1,0:T(8,128)} %get-tuple-element.38.refs_5_), channel_id=1, source_target_pairs={{0,1},{1,0},{2,3},{3,2},{4,5},{5,4},{6,7},{7,6},{8,9},{9,8},{10,11... | collective-permute-start | bytes 73736 | tf_op jit(solution)/shard_map/ppermute | solution.py:574
  5.0 18.4 %collective-permute-start.1 = (f32[6,8,128]{2,1,0:T(8,128)}, f32[6,8,128]{2,1,0:T(8,128)S(1)}, u32[]{:S(2)}, u32[]{:S(2)}) collective-permute-start(f32[6,8,128]{2,1,0:T(8,128)} %get-tuple-element.39.refs_6_), channel_id=1, source_target_pairs={{0,73},{1,8},{2,75},{3,10},{4,77},{5,12},{6,79},{7,14},{8,1},{9,64... | collective-permute-start | bytes 73736 | tf_op jit(solution)/shard_map/ppermute | solution.py:574
  9.7 13.6 %collective-permute-start.2 = (f32[6,8,128]{2,1,0:T(8,128)}, f32[6,8,128]{2,1,0:T(8,128)S(1)}, u32[]{:S(2)}, u32[]{:S(2)}) collective-permute-start(f32[6,8,128]{2,1,0:T(8,128)} %get-tuple-element.40.refs_7_), channel_id=1, source_target_pairs={{0,2},{1,3},{2,0},{3,1},{4,6},{5,7},{6,4},{7,5},{8,10},{9,11},{10,... | collective-permute-start | bytes 73736 | tf_op jit(solution)/shard_map/ppermute | solution.py:574
  11.2 12.2 %collective-permute-start.3 = (f32[6,8,128]{2,1,0:T(8,128)}, f32[6,8,128]{2,1,0:T(8,128)S(1)}, u32[]{:S(2)}, u32[]{:S(2)}) collective-permute-start(f32[6,8,128]{2,1,0:T(8,128)} %get-tuple-element.41.refs_8_), channel_id=1, source_target_pairs={{0,18},{1,19},{2,16},{3,17},{4,22},{5,23},{6,20},{7,21},{8,26},{9,... | collective-permute-start | bytes 73736 | tf_op jit(solution)/shard_map/ppermute | solution.py:574
  14.8 8.6 %collective-permute-start.4 = (f32[6,8,128]{2,1,0:T(8,128)}, f32[6,8,128]{2,1,0:T(8,128)S(1)}, u32[]{:S(2)}, u32[]{:S(2)}) collective-permute-start(f32[6,8,128]{2,1,0:T(8,128)} %get-tuple-element.42.refs_9_), channel_id=1, source_target_pairs={{0,4},{1,5},{2,6},{3,7},{4,0},{5,1},{6,2},{7,3},{8,12},{9,13},{10,... | collective-permute-start | bytes 73736 | tf_op jit(solution)/shard_map/ppermute | solution.py:574
  17.8 2.3 %copy-start.2 = (f32[6,8,128]{2,1,0:T(8,128)}, f32[6,8,128]{2,1,0:T(8,128)S(1)}, u32[]{:S(2)}) copy-start(f32[6,8,128]{2,1,0:T(8,128)S(1)} %collective-permute-done.refs_11_) | copy-start | bytes 73732
  17.8 6.4 %collective-permute-start.5 = (f32[6,8,128]{2,1,0:T(8,128)}, f32[6,8,128]{2,1,0:T(8,128)S(1)}, u32[]{:S(2)}, u32[]{:S(2)}) collective-permute-start(f32[6,8,128]{2,1,0:T(8,128)} %get-tuple-element.43.refs_10_), channel_id=1, source_target_pairs={{0,36},{1,37},{2,38},{3,39},{4,32},{5,33},{6,34},{7,35},{8,44},{9,... | collective-permute-start | bytes 73736 | tf_op jit(solution)/shard_map/ppermute | solution.py:574
  23.4 0.9 %copy-start.3 = (f32[6,8,128]{2,1,0:T(8,128)}, f32[6,8,128]{2,1,0:T(8,128)S(1)}, u32[]{:S(2)}) copy-start(f32[6,8,128]{2,1,0:T(8,128)S(1)} %collective-permute-done.1.refs_12_) | copy-start | bytes 73732
  23.4 0.9 %copy-start.4 = (f32[6,8,128]{2,1,0:T(8,128)}, f32[6,8,128]{2,1,0:T(8,128)S(1)}, u32[]{:S(2)}) copy-start(f32[6,8,128]{2,1,0:T(8,128)S(1)} %collective-permute-done.2.refs_13_) | copy-start | bytes 73732
  23.4 0.8 %copy-start.5 = (f32[6,8,128]{2,1,0:T(8,128)}, f32[6,8,128]{2,1,0:T(8,128)S(1)}, u32[]{:S(2)}) copy-start(f32[6,8,128]{2,1,0:T(8,128)S(1)} %collective-permute-done.3.refs_14_) | copy-start | bytes 73732
  28.0 5.7 %collective-permute-start.10 = (f32[5,8,128]{2,1,0:T(8,128)}, f32[5,8,128]{2,1,0:T(8,128)S(1)}, u32[]{:S(2)}, u32[]{:S(2)}) collective-permute-start(f32[5,8,128]{2,1,0:T(8,128)} %get-tuple-element.49.refs_9_), channel_id=1, source_target_pairs={{0,4},{1,5},{2,6},{3,7},{4,0},{5,1},{6,2},{7,3},{8,12},{9,13},{10,... | collective-permute-start | bytes 61448 | tf_op jit(solution)/shard_map/ppermute | solution.py:574
  30.9 7.0 %collective-permute-start.11 = (f32[5,8,128]{2,1,0:T(8,128)}, f32[5,8,128]{2,1,0:T(8,128)S(1)}, u32[]{:S(2)}, u32[]{:S(2)}) collective-permute-start(f32[5,8,128]{2,1,0:T(8,128)} %get-tuple-element.50.refs_10_), channel_id=1, source_target_pairs={{0,36},{1,37},{2,38},{3,39},{4,32},{5,33},{6,34},{7,35},{8,44},{9,... | collective-permute-start | bytes 61448 | tf_op jit(solution)/shard_map/ppermute | solution.py:574
  32.2 5.7 %collective-permute-start.6 = (f32[5,8,128]{2,1,0:T(8,128)}, f32[5,8,128]{2,1,0:T(8,128)S(1)}, u32[]{:S(2)}, u32[]{:S(2)}) collective-permute-start(f32[5,8,128]{2,1,0:T(8,128)} %get-tuple-element.45.refs_5_), channel_id=1, source_target_pairs={{0,1},{1,0},{2,3},{3,2},{4,5},{5,4},{6,7},{7,6},{8,9},{9,8},{10,11... | collective-permute-start | bytes 61448 | tf_op jit(solution)/shard_map/ppermute | solution.py:574
  32.2 5.9 %collective-permute-start.7 = (f32[5,8,128]{2,1,0:T(8,128)}, f32[5,8,128]{2,1,0:T(8,128)S(1)}, u32[]{:S(2)}, u32[]{:S(2)}) collective-permute-start(f32[5,8,128]{2,1,0:T(8,128)} %get-tuple-element.46.refs_6_), channel_id=1, source_target_pairs={{0,73},{1,8},{2,75},{3,10},{4,77},{5,12},{6,79},{7,14},{8,1},{9,64... | collective-permute-start | bytes 61448 | tf_op jit(solution)/shard_map/ppermute | solution.py:574
  32.3 5.9 %collective-permute-start.8 = (f32[5,8,128]{2,1,0:T(8,128)}, f32[5,8,128]{2,1,0:T(8,128)S(1)}, u32[]{:S(2)}, u32[]{:S(2)}) collective-permute-start(f32[5,8,128]{2,1,0:T(8,128)} %get-tuple-element.47.refs_7_), channel_id=1, source_target_pairs={{0,2},{1,3},{2,0},{3,1},{4,6},{5,7},{6,4},{7,5},{8,10},{9,11},{10,... | collective-permute-start | bytes 61448 | tf_op jit(solution)/shard_map/ppermute | solution.py:574
  33.7 4.2 %copy-start.8 = (f32[5,8,128]{2,1,0:T(8,128)}, f32[5,8,128]{2,1,0:T(8,128)S(1)}, u32[]{:S(2)}) copy-start(f32[5,8,128]{2,1,0:T(8,128)S(1)} %collective-permute-done.10.refs_15_) | copy-start | bytes 61444
  33.7 6.4 %collective-permute-start.9 = (f32[5,8,128]{2,1,0:T(8,128)}, f32[5,8,128]{2,1,0:T(8,128)S(1)}, u32[]{:S(2)}, u32[]{:S(2)}) collective-permute-start(f32[5,8,128]{2,1,0:T(8,128)} %get-tuple-element.48.refs_8_), channel_id=1, source_target_pairs={{0,18},{1,19},{2,16},{3,17},{4,22},{5,23},{6,20},{7,21},{8,26},{9,... | collective-permute-start | bytes 61448 | tf_op jit(solution)/shard_map/ppermute | solution.py:574
  37.9 2.2 %copy-start.9 = (f32[5,8,128]{2,1,0:T(8,128)}, f32[5,8,128]{2,1,0:T(8,128)S(1)}, u32[]{:S(2)}) copy-start(f32[5,8,128]{2,1,0:T(8,128)S(1)} %collective-permute-done.11.refs_16_) | copy-start | bytes 61444
  37.9 2.2 %copy-start.10 = (f32[5,8,128]{2,1,0:T(8,128)}, f32[5,8,128]{2,1,0:T(8,128)S(1)}, u32[]{:S(2)}) copy-start(f32[5,8,128]{2,1,0:T(8,128)S(1)} %collective-permute-done.6.refs_11_) | copy-start | bytes 61444
  38.1 2.0 %copy-start.11 = (f32[5,8,128]{2,1,0:T(8,128)}, f32[5,8,128]{2,1,0:T(8,128)S(1)}, u32[]{:S(2)}) copy-start(f32[5,8,128]{2,1,0:T(8,128)S(1)} %collective-permute-done.7.refs_12_) | copy-start | bytes 61444
  38.2 2.0 %copy-start.12 = (f32[5,8,128]{2,1,0:T(8,128)}, f32[5,8,128]{2,1,0:T(8,128)S(1)}, u32[]{:S(2)}) copy-start(f32[5,8,128]{2,1,0:T(8,128)S(1)} %collective-permute-done.8.refs_13_) | copy-start | bytes 61444
  43.8 9.3 %collective-permute-start.12 = (f32[5,8,128]{2,1,0:T(8,128)}, f32[5,8,128]{2,1,0:T(8,128)S(1)}, u32[]{:S(2)}, u32[]{:S(2)}) collective-permute-start(f32[5,8,128]{2,1,0:T(8,128)} %get-tuple-element.58.refs_4_), channel_id=1, source_target_pairs={{0,1},{1,0},{2,3},{3,2},{4,5},{5,4},{6,7},{7,6},{8,9},{9,8},{10,11... | collective-permute-start | bytes 61448 | tf_op jit(solution)/shard_map/ppermute | solution.py:574
  43.9 14.7 %collective-permute-start.13 = (f32[5,8,128]{2,1,0:T(8,128)}, f32[5,8,128]{2,1,0:T(8,128)S(1)}, u32[]{:S(2)}, u32[]{:S(2)}) collective-permute-start(f32[5,8,128]{2,1,0:T(8,128)} %get-tuple-element.59.refs_5_), channel_id=1, source_target_pairs={{0,73},{1,8},{2,75},{3,10},{4,77},{5,12},{6,79},{7,14},{8,1},{9,64... | collective-permute-start | bytes 61448 | tf_op jit(solution)/shard_map/ppermute | solution.py:574
  46.7 15.1 %collective-permute-start.14 = (f32[5,8,128]{2,1,0:T(8,128)}, f32[5,8,128]{2,1,0:T(8,128)S(1)}, u32[]{:S(2)}, u32[]{:S(2)}) collective-permute-start(f32[5,8,128]{2,1,0:T(8,128)} %get-tuple-element.60.refs_6_), channel_id=1, source_target_pairs={{0,2},{1,3},{2,0},{3,1},{4,6},{5,7},{6,4},{7,5},{8,10},{9,11},{10,... | collective-permute-start | bytes 61448 | tf_op jit(solution)/shard_map/ppermute | solution.py:574
  47.5 14.2 %collective-permute-start.15 = (f32[5,8,128]{2,1,0:T(8,128)}, f32[5,8,128]{2,1,0:T(8,128)S(1)}, u32[]{:S(2)}, u32[]{:S(2)}) collective-permute-start(f32[5,8,128]{2,1,0:T(8,128)} %get-tuple-element.61.refs_7_), channel_id=1, source_target_pairs={{0,18},{1,19},{2,16},{3,17},{4,22},{5,23},{6,20},{7,21},{8,26},{9,... | collective-permute-start | bytes 61448 | tf_op jit(solution)/shard_map/ppermute | solution.py:574
  50.1 11.7 %collective-permute-start.16 = (f32[5,8,128]{2,1,0:T(8,128)}, f32[5,8,128]{2,1,0:T(8,128)S(1)}, u32[]{:S(2)}, u32[]{:S(2)}) collective-permute-start(f32[5,8,128]{2,1,0:T(8,128)} %get-tuple-element.62.refs_8_), channel_id=1, source_target_pairs={{0,4},{1,5},{2,6},{3,7},{4,0},{5,1},{6,2},{7,3},{8,12},{9,13},{10,... | collective-permute-start | bytes 61448 | tf_op jit(solution)/shard_map/ppermute | solution.py:574
  53.1 2.6 %copy-start.14 = (f32[5,8,128]{2,1,0:T(8,128)}, f32[5,8,128]{2,1,0:T(8,128)S(1)}, u32[]{:S(2)}) copy-start(f32[5,8,128]{2,1,0:T(8,128)S(1)} %collective-permute-done.12.refs_10_) | copy-start | bytes 61444
  53.1 8.7 %collective-permute-start.17 = (f32[5,8,128]{2,1,0:T(8,128)}, f32[5,8,128]{2,1,0:T(8,128)S(1)}, u32[]{:S(2)}, u32[]{:S(2)}) collective-permute-start(f32[5,8,128]{2,1,0:T(8,128)} %get-tuple-element.63.refs_9_), channel_id=1, source_target_pairs={{0,36},{1,37},{2,38},{3,39},{4,32},{5,33},{6,34},{7,35},{8,44},{9,... | collective-permute-start | bytes 61448 | tf_op jit(solution)/shard_map/ppermute | solution.py:574
  58.6 3.1 %copy-start.15 = (f32[5,8,128]{2,1,0:T(8,128)}, f32[5,8,128]{2,1,0:T(8,128)S(1)}, u32[]{:S(2)}) copy-start(f32[5,8,128]{2,1,0:T(8,128)S(1)} %collective-permute-done.13.refs_11_) | copy-start | bytes 61444
  58.6 9.2 %collective-permute-start.18 = (f32[6,4,512]{2,1,0:T(4,128)}, f32[6,4,512]{2,1,0:T(4,128)S(1)}, u32[]{:S(2)}, u32[]{:S(2)}) collective-permute-start(f32[6,4,512]{2,1,0:T(4,128)} %get-tuple-element.65), channel_id=1, source_target_pairs={{0,1},{1,2},{2,3},{3,4},{4,5},{5,6},{6,7},{7,8},{8,9},{9,10},{10,1... | collective-permute-start | bytes 147464 | tf_op jit(solution)/shard_map/ppermute | solution.py:643
  65.5 9.1 %collective-permute-start.19 = (f32[5,4,512]{2,1,0:T(4,128)}, f32[5,4,512]{2,1,0:T(4,128)S(1)}, u32[]{:S(2)}, u32[]{:S(2)}) collective-permute-start(f32[5,4,512]{2,1,0:T(4,128)} %get-tuple-element.66), channel_id=1, source_target_pairs={{0,1},{1,2},{2,3},{3,4},{4,5},{5,6},{6,7},{7,8},{8,9},{9,10},{10,1... | collective-permute-start | bytes 122888 | tf_op jit(solution)/shard_map/ppermute | solution.py:644
  67.8 6.8 %copy-start = (f32[6,4,512]{2,1,0:T(4,128)}, f32[6,4,512]{2,1,0:T(4,128)S(1)}, u32[]{:S(2)}) copy-start(f32[6,4,512]{2,1,0:T(4,128)S(1)} %collective-permute-done.18.state_ref) | copy-start | bytes 147460
  (9 other events, 5.7 us)
where the time goes:
time: 77.4 us; the launch traced here: 76.9 us
  starting transfers between devices  31.6 us (41%)
  Pallas kernels  29.3 us (38%)
  waiting for transfers between devices  10.7 us (14%)
  local copies, waits for them, and re-layouts  4.39 us (6%)
  between operations  0.84 us (1%)
    ppermute x18, starting transfers between devices, exchange(): ghosts[number] = lax.ppermute(messages[number], AXIS, swaps[number])  30.2 us
    pallas_call x11, Pallas kernels, call(): pl.pallas_call(kernel, out_shape=outs, in_specs=specs, out_specs=[vmem] *...  29.3 us
    ppermute x1, waiting for transfers between devices, local(): got_res = lax.ppermute(sent_res, AXIS, forward)  6.79 us
    unnamed x43, local copies, waits for them, and re-layouts  4.39 us
    ppermute x18, waiting for transfers between devices, exchange(): ghosts[number] = lax.ppermute(messages[number], AXIS, swaps[number])  2.98 us
  transfers between devices with their start and end apart: 20, of which 5 were waited for; matrix products, arithmetic and copies ran while one was open for 0% of the time, Pallas kernels for 24%

commit v1 on v0

--- a/solution.py
+++ b/solution.py
@@ -319,48 +319,60 @@
     return jnp.sum(jnp.where(same, row, 0), axis=1, keepdims=True)
 
 
-def brick_lane(device, neighbour_ref, parent_column):
-    outside = (neighbour_ref[...] >> 6) != device
-    outside = outside.astype(I32)
+def brick_lane(device, neighbour, parent):
+    outside = ((neighbour >> 6) != device).astype(I32)
     place = []
     for direction in range(3):
-        odd = parent_column >> (2 - direction) & 1
+        odd = parent >> (2 - direction) & 1
         upper = jnp.where(
             odd == 1,
-            outside[:, 2 * direction + 1 : 2 * direction + 2],
-            1 - outside[:, 2 * direction : 2 * direction + 1],
+            outside[2 * direction + 1 : 2 * direction + 2],
+            1 - outside[2 * direction : 2 * direction + 1],
         )
         place.append(odd + 2 * upper)
     return place[1] * 32 + place[2] * 8 + place[0] * 2
 
 
-def prepare_kernel(count, device_ref, state_ref, volume_ref, neighbour_ref, parent_ref, *outs):
-    u_ref, frac_ref = outs[0:2]
-    message_refs = outs[2:8]
+def prepare_kernel(count, device_ref, state_hbm, volume_hbm, neighbour_hbm, parent_hbm, *refs):
+    u_ref, frac_ref = refs[0:2]
+    message_refs = refs[2:8]
+    state_ref, volume_ref, neighbour_ref, parent_ref, sems = refs[8:13]
+    copies = [
+        pltpu.make_async_copy(neighbour_hbm, neighbour_ref, sems.at[0]),
+        pltpu.make_async_copy(parent_hbm, parent_ref, sems.at[1]),
+        pltpu.make_async_copy(volume_hbm, volume_ref, sems.at[2]),
+    ]
+    for q in range(5):
+        copies.append(pltpu.make_async_copy(state_hbm.at[q], state_ref.at[q], sems.at[3 + q]))
+    for copy in copies:
+        copy.start()
     device, even, _ = cube_place(device_ref, count)
-    lane = brick_lane(device, neighbour_ref, as_column(parent_ref[...], 64))
+    copies[0].wait()
+    copies[1].wait()
+    lane = as_column(brick_lane(device, neighbour_ref[...], parent_ref[...]), 64)
     spread = [
         (lane_index((64, LANES)) == lane + half).astype(F32).astype(BF16) for half in (0, 1)
     ]
     tripled = [jnp.concatenate([s, s, s], axis=0) for s in spread]
     dims = (((0,), (0,)), ((), ()))
+    copies[2].wait()
+    volume = (volume_ref[...].astype(F32) / 8.0).astype(BF16)
+    frac_ref[...] = lax.dot_general(
+        volume[:, 0:256], spread[0], dims, preferred_element_type=F32
+    ) + lax.dot_general(volume[:, 256:512], spread[1], dims, preferred_element_type=F32)
     for q in range(5):
+        copies[3 + q].wait()
         parts = jnp.concatenate(split3(state_ref[q]), axis=0)
         u_ref[q] = lax.dot_general(
             parts[:, 0:256], tripled[0], dims, preferred_element_type=F32
         ) + lax.dot_general(parts[:, 256:512], tripled[1], dims, preferred_element_type=F32)
-    volume = (volume_ref[...].astype(F32) / 8.0).astype(BF16)
-    frac_ref[...] = lax.dot_general(
-        volume[:, 0:256], spread[0], dims, preferred_element_type=F32
-    ) + lax.dot_general(volume[:, 256:512], spread[1], dims, preferred_element_type=F32)
     write_messages([(u_ref, (q,)) for q in range(5)] + [(frac_ref, ())], message_refs, even)
 
 
-def tables_kernel(count, device_ref, neighbour_ref, parent_ref, spread_ref, order_ref, pick_ref):
+def tables_kernel(device_ref, neighbour_ref, parent_ref, spread_ref, order_ref, pick_ref):
     device = device_ref[0]
-    parent_row = parent_ref[...]
-    parent_column = as_column(parent_row, 64)
-    lane = brick_lane(device, neighbour_ref, parent_column)
+    parent_column = as_column(parent_ref[...], 64)
+    lane = as_column(brick_lane(device, neighbour_ref[...], parent_ref[...]), 64)
     lanes = lane_index((64, LANES))
     spread = [(lanes == lane + half).astype(F32) for half in (0, 1)]
     spread_ref[0] = spread[0]
@@ -476,20 +488,9 @@
     return jnp.concatenate([order, order, order], axis=1)
 
 
-def state_kernel(u_ref, frac_ref, spread_ref, order_ref, out_ref, kept_ref, sent_ref, rows_ref, half_ref):
+def state_kernel(u_ref, frac_ref, order_ref, kept_ref, sent_ref, rows_ref, half_ref):
     rows_ref[...] = jnp.zeros_like(rows_ref)
-    tripled = []
-    for half in (0, 1):
-        spread = spread_ref[half].astype(BF16)
-        tripled.append(jnp.concatenate([spread, spread, spread], axis=1))
     order3 = tripled_order(order_ref)
-    dims = (((1,), (1,)), ((), ()))
-    for q in range(5):
-        parts = jnp.concatenate(split3(u_ref[q]), axis=1)
-        for half in (0, 1):
-            out_ref[q, :, pl.ds(half * 256, 256)] = lax.dot_general(
-                tripled[half], parts, dims, preferred_element_type=F32
-            )
     for q in range(6):
         if q < 5:
             def registers(i, iy, q=q):
@@ -503,10 +504,24 @@
         sent_ref[q] = sums[4:8]
 
 
+def output_kernel(u_ref, spread_ref, out_ref):
+    tripled = []
+    for half in (0, 1):
+        spread = spread_ref[half].astype(BF16)
+        tripled.append(jnp.concatenate([spread, spread, spread], axis=1))
+    dims = (((1,), (1,)), ((), ()))
+    for q in range(5):
+        parts = jnp.concatenate(split3(u_ref[q]), axis=1)
+        for half in (0, 1):
+            out_ref[q, :, pl.ds(half * 256, 256)] = lax.dot_general(
+                tripled[half], parts, dims, preferred_element_type=F32
+            )
+
+
 def residual_kernel(count, device_ref, *refs):
-    inner_ref, faces_ref, order_ref = refs[0:3]
-    own_refs, ghost_refs = refs[3:9], refs[9:15]
-    kept_ref, sent_ref, res_ref, rows_ref, half_ref = refs[15:20]
+    inner_ref, faces_ref, order_ref, sent_state_ref = refs[0:4]
+    own_refs, ghost_refs = refs[4:10], refs[10:16]
+    kept_ref, sent_ref, res_ref, rows_ref, half_ref = refs[16:21]
     _, even, far = cube_place(device_ref, count)
     res_ref[...] = inner_ref[...]
     boundary_body(
@@ -525,42 +540,56 @@
             lambda i, iy: res_ref[q, place_of_register(i, iy), :], order3, rows_ref, half_ref
         )
         kept_ref[q] = sums[0:4]
-        sent_ref[q] = sums[4:8]
-
-
-def coarse_kernel(pick_ref, kept_state_ref, kept_res_ref, state_ref, res_ref, out_state_ref, out_res_ref):
+        sent_ref[6 + q] = sums[4:8]
+    sent_ref[0:6] = sent_state_ref[...]
+
+
+def coarse_kernel(pick_ref, kept_state_ref, kept_res_ref, got_ref, out_state_ref, out_res_ref):
     pick = pick_ref[...]
+    chosen = [jnp.broadcast_to(pick[:, source : source + 1], (8, 512)) > 0.5 for source in range(8)]
 
     def choose(kept, received):
         result = None
         for source in range(8):
             row = kept[source : source + 1] if source < 4 else received[source - 4 : source - 3]
-            piece = jnp.where(pick[:, source : source + 1] > 0.5, row, 0.0)
-            result = piece if result is None else result + piece
+            row = jnp.broadcast_to(row, (8, 512))
+            result = row if result is None else jnp.where(chosen[source], row, result)
         return result
 
-    weight = choose(kept_state_ref[5], state_ref[5])
+    weight = choose(kept_state_ref[5], got_ref[5])
     for q in range(5):
-        out_state_ref[q] = choose(kept_state_ref[q], state_ref[q]) / weight
-        out_res_ref[q] = choose(kept_res_ref[q], res_ref[q])
+        out_state_ref[q] = choose(kept_state_ref[q], got_ref[q]) / weight
+        out_res_ref[q] = choose(kept_res_ref[q], got_ref[6 + q])
 
 
 def f32(*shape):
     return jax.ShapeDtypeStruct(shape, F32)
 
 
-def call(kernel, outs, scratch, args, name, smem=1):
+def held(*shape):
+    return pltpu.VMEM(shape, F32)
+
+
+def call(kernel, outs, scratch, args, smem=1, sources=0):
     vmem = pl.BlockSpec(memory_space=pltpu.VMEM)
-    specs = [pl.BlockSpec(memory_space=pltpu.SMEM)] * smem + [vmem] * (len(args) - smem)
+    spaces = [pltpu.SMEM] * smem + [pltpu.HBM] * sources
+    spaces += [pltpu.VMEM] * (len(args) - len(spaces))
+    args = [
+        pltpu.with_memory_space_constraint(arg, space) if space is not pltpu.SMEM else arg
+        for arg, space in zip(args, spaces)
+    ]
     return pl.pallas_call(
         kernel,
         out_shape=outs,
-        in_specs=specs,
+        in_specs=[pl.BlockSpec(memory_space=space) for space in spaces],
         out_specs=[vmem] * len(outs),
-        scratch_shapes=[pltpu.VMEM(shape, F32) for shape in scratch],
-        name=name,
+        scratch_shapes=[pltpu.VMEM(item, F32) if isinstance(item, tuple) else item for item in scratch],
+        compiler_params=pltpu.CompilerParams(vmem_limit_bytes=8 << 20),
         cost_estimate=pl.CostEstimate(flops=8_000_000, bytes_accessed=4_000_000, transcendentals=0),
     )(*args)
+
+
+START_ORDER = (5, 3, 1, 4, 2, 0)
 
 
 def solution(mesh):
@@ -570,84 +599,85 @@
 
     def exchange(messages):
         ghosts = [None] * 6
-        for number in (5, 3, 1, 4, 2, 0):
+        for number in START_ORDER:
             ghosts[number] = lax.ppermute(messages[number], AXIS, swaps[number])
         return ghosts
 
-    def interior(u, frac, with_speed, name):
+    def interior(u, frac, with_speed):
         rows = 6 if with_speed else 5
         return call(
             lambda *refs: interior_kernel(with_speed, *refs),
-            [f32(rows, ROWS, LANES)],
+            [held(rows, ROWS, LANES)],
             [(5, ROWS, LANES), (rows, 64, LANES)],
             [u, frac],
-            name,
             0,
         )[0]
 
     def local(state, volume, neighbour, parent):
         device = lax.axis_index(AXIS).astype(I32).reshape(1)
         parent = parent.reshape(1, 64)
-        grid = f32(5, ROWS, LANES)
+        neighbour = neighbour.T
+        grid = held(5, ROWS, LANES)
         u, frac, *sent = call(
             lambda *refs: prepare_kernel(count, *refs),
-            [grid, f32(ROWS, LANES)] + [f32(6, 8, LANES)] * 6,
-            [],
+            [grid, held(ROWS, LANES)] + [held(6, 8, LANES)] * 6,
+            [
+                (5, 64, 512),
+                pltpu.VMEM((64, 512), I32),
+                pltpu.VMEM((6, 64), I32),
+                pltpu.VMEM((1, 64), I32),
+                pltpu.SemaphoreType.DMA((8,)),
+            ],
             [device, state, volume, neighbour, parent],
-            "prepare",
+            1,
+            4,
         )
         ghosts = exchange(sent)
         spread, order, pick = call(
-            lambda *refs: tables_kernel(count, *refs),
-            [f32(2, 64, LANES), f32(LANES, LANES), f32(8, LANES)],
+            lambda *refs: tables_kernel(*refs),
+            [held(2, 64, LANES), held(LANES, LANES), held(8, LANES)],
             [],
             [device, neighbour, parent],
-            "tables",
-        )
-        mix = call(mixing_kernel, [f32(ROWS, LANES)], [], [frac], "mixing", 0)[0]
-        inner = interior(u, frac, True, "interior_1")
+        )
+        mix = call(mixing_kernel, [held(ROWS, LANES)], [], [frac], 0)[0]
+        inner = interior(u, frac, True)
         middle, *rest = call(
             lambda *refs: update_kernel(count, True, *refs),
-            [grid] + [f32(5, 8, LANES)] * 6 + [f32(6, 8, LANES)],
+            [grid] + [held(5, 8, LANES)] * 6 + [held(6, 8, LANES)],
             [(6, ROWS, LANES)],
             [device, u, frac, mix, inner, *sent, *ghosts],
-            "update_1",
         )
         sent, faces = rest[0:6], rest[6]
         ghosts = exchange(sent)
-        inner = interior(middle, frac, True, "interior_2")
+        inner = interior(middle, frac, True)
         fine, *sent = call(
             lambda *refs: update_kernel(count, False, *refs),
-            [grid] + [f32(5, 8, LANES)] * 6,
+            [grid] + [held(5, 8, LANES)] * 6,
             [(6, ROWS, LANES)],
             [device, u, frac, mix, inner, *sent, *ghosts, faces],
-            "update_2",
         )
         ghosts = exchange(sent)
-        inner = interior(fine, frac, False, "interior_3")
-        fine_out, kept_state, sent_state = call(
+        inner = interior(fine, frac, False)
+        kept_state, sent_state = call(
             state_kernel,
-            [f32(5, 64, 512), f32(6, 4, 512), f32(6, 4, 512)],
+            [held(6, 4, 512), held(6, 4, 512)],
             [(LANES, LANES), (64, LANES)],
-            [fine, frac, spread, order],
-            "restrict_state",
+            [fine, frac, order],
             0,
         )
-        kept_res, sent_res = call(
+        kept_res, outgoing = call(
             lambda *refs: residual_kernel(count, *refs),
-            [f32(5, 4, 512), f32(5, 4, 512)],
+            [held(5, 4, 512), held(11, 4, 512)],
             [(5, ROWS, LANES), (LANES, LANES), (64, LANES)],
-            [device, inner, faces, order, *sent, *ghosts],
-            "restrict_residual",
-        )
-        got_state = lax.ppermute(sent_state, AXIS, forward)
-        got_res = lax.ppermute(sent_res, AXIS, forward)
+            [device, inner, faces, order, sent_state, *sent, *ghosts],
+        )
+        got = lax.ppermute(outgoing, AXIS, forward)
+        fine_out = call(output_kernel, [f32(5, 64, 512)], [], [fine, spread], 0)[0]
         coarse_state, coarse_residual = call(
             coarse_kernel,
             [f32(5, 8, 512), f32(5, 8, 512)],
             [],
-            [pick, kept_state, kept_res, got_state, got_res],
-            "coarse",
+            [pick, kept_state, kept_res, got],
             0,
         )
         return fine_out, coarse_state, coarse_residual

time: 77.4 us -> 59.1 us (0.76)
  Pallas kernels: 29.3 us -> 12.2 us
  waiting for transfers between devices: 10.7 us -> 17.7 us
  local copies, waits for them, and re-layouts: 4.39 us -> 0.01 us
  starting transfers between devices: 31.6 us -> 28.4 us
    pallas_call x11 -> x12, Pallas kernels: 29.3 us -> 12.2 us  [call(): pl.pallas_call(kernel, out_shape=outs, in_specs=[pl.BlockSpec(memory_spac...]
    ppermute x18, waiting for transfers between devices: 2.98 us -> 9.89 us  [exchange(): ghosts[number] = lax.ppermute(messages[number], AXIS, swaps[number])]
    unnamed x43 -> x4, local copies, waits for them, and re-layouts: 4.39 us -> 0.01 us
    ppermute x18, starting transfers between devices: 30.2 us -> 28.3 us  [exchange(): ghosts[number] = lax.ppermute(messages[number], AXIS, swaps[number])]
    ppermute x2 -> x1, starting transfers between devices: 1.4 us -> 0.07 us  [local(): got = lax.ppermute(outgoing, AXIS, forward)]
    ppermute x2 -> x1, waiting for transfers between devices: 7.71 us -> 7.78 us  [local(): got = lax.ppermute(outgoing, AXIS, forward)]
  transfers between devices with their start and end apart: 20 -> 19, of which waited for: 5 -> 7; matrix products, arithmetic and copies ran while one was open for 0% -> 0% of each run, Pallas kernels for 24% -> 11%
where the time goes in v1:
time: 59.1 us; the launch traced here: 59 us
  starting transfers between devices  28.4 us (48%)
  waiting for transfers between devices  17.7 us (30%)
  Pallas kernels  12.2 us (21%)
  between operations  0.8 us (1%)
    ppermute x18, starting transfers between devices, exchange(): ghosts[number] = lax.ppermute(messages[number], AXIS, swaps[number])  28.3 us
    pallas_call x12, Pallas kernels, call(): pl.pallas_call(kernel, out_shape=outs, in_specs=[pl.BlockSpec(memory_spac...  12.2 us
    ppermute x18, waiting for transfers between devices, exchange(): ghosts[number] = lax.ppermute(messages[number], AXIS, swaps[number])  9.89 us
    ppermute x1, waiting for transfers between devices, local(): got = lax.ppermute(outgoing, AXIS, forward)  7.78 us
  transfers between devices with their start and end apart: 19, of which 7 were waited for; matrix products, arithmetic and copies ran while one was open for 0% of the time, Pallas kernels for 11%

profile of v1, /device:TPU:0, one launch (start us, length us, event | category | flops | bytes accessed | tf_op | source)
XLA Modules:
  0.0 59.0 jit_solution(17343484844127281514)
XLA Ops:
  0.6 2.9 %shard_map.67 = (f32[5,256,128]{2,1,0:T(8,128)S(1)}, f32[256,128]{1,0:T(8,128)S(1)}, f32[6,8,128]{2,1,0:T(8,128)S(1)}, f32[6,8,128]{2,1,0:T(8,128)S(1)}, f32[6,8...) custom-call(s32[1]{0:T(128)} %bitcast.refs_0_, ...), custom_call_target="tpu_custom_call" | custom-call | flops 8000000 | bytes 4000000 | tf_op jit(solution)/shard_map/pallas_call | solution.py:581
  3.6 4.8 %collective-permute-start.1 = (f32[6,8,128]{2,1,0:T(8,128)S(1)}, f32[6,8,128]{2,1,0:T(8,128)S(1)}, u32[]{:S(2)}, u32[]{:S(2)}) collective-permute-start(f32[6,8,128]{2,1,0:T(8,128)S(1)} %get-tuple-element.38.refs_6_), channel_id=1, source_target_pairs={{0,73},{1,8},{2,75},{3,10},{4,77},{5,12},{6,79},{7,14},{8,1},{9,64... | collective-permute-start | bytes 73736 | tf_op jit(solution)/shard_map/ppermute | solution.py:603
  8.4 1.5 %collective-permute-start.2 = (f32[6,8,128]{2,1,0:T(8,128)S(1)}, f32[6,8,128]{2,1,0:T(8,128)S(1)}, u32[]{:S(2)}, u32[]{:S(2)}) collective-permute-start(f32[6,8,128]{2,1,0:T(8,128)S(1)} %get-tuple-element.39.refs_7_), channel_id=1, source_target_pairs={{0,2},{1,3},{2,0},{3,1},{4,6},{5,7},{6,4},{7,5},{8,10},{9,11},{10,... | collective-permute-start | bytes 73736 | tf_op jit(solution)/shard_map/ppermute | solution.py:603
  9.9 3.6 %collective-permute-start.3 = (f32[6,8,128]{2,1,0:T(8,128)S(1)}, f32[6,8,128]{2,1,0:T(8,128)S(1)}, u32[]{:S(2)}, u32[]{:S(2)}) collective-permute-start(f32[6,8,128]{2,1,0:T(8,128)S(1)} %get-tuple-element.40.refs_8_), channel_id=1, source_target_pairs={{0,18},{1,19},{2,16},{3,17},{4,22},{5,23},{6,20},{7,21},{8,26},{9,... | collective-permute-start | bytes 73736 | tf_op jit(solution)/shard_map/ppermute | solution.py:603
  13.4 3.0 %collective-permute-start.4 = (f32[6,8,128]{2,1,0:T(8,128)S(1)}, f32[6,8,128]{2,1,0:T(8,128)S(1)}, u32[]{:S(2)}, u32[]{:S(2)}) collective-permute-start(f32[6,8,128]{2,1,0:T(8,128)S(1)} %get-tuple-element.41.refs_9_), channel_id=1, source_target_pairs={{0,4},{1,5},{2,6},{3,7},{4,0},{5,1},{6,2},{7,3},{8,12},{9,13},{10,... | collective-permute-start | bytes 73736 | tf_op jit(solution)/shard_map/ppermute | solution.py:603
  16.5 0.6 %collective-permute-start.5 = (f32[6,8,128]{2,1,0:T(8,128)S(1)}, f32[6,8,128]{2,1,0:T(8,128)S(1)}, u32[]{:S(2)}, u32[]{:S(2)}) collective-permute-start(f32[6,8,128]{2,1,0:T(8,128)S(1)} %get-tuple-element.42.refs_10_), channel_id=1, source_target_pairs={{0,36},{1,37},{2,38},{3,39},{4,32},{5,33},{6,34},{7,35},{8,44},{9,... | collective-permute-start | bytes 73736 | tf_op jit(solution)/shard_map/ppermute | solution.py:603
  17.2 1.3 %shard_map.69.refs_4_ = f32[6,256,128]{2,1,0:T(8,128)S(1)} custom-call(f32[5,256,128]{2,1,0:T(8,128)S(1)} %get-tuple-element.35.refs_0_.refs_1_, f32[256,128]{1,0:T(8,128)S(1)} %get-tuple-element.36.frac_ref.refs_1_.refs_2_), custom_call_target="tpu_custom_call" | custom-call | flops 8000000 | bytes 4000000 | tf_op jit(solution)/shard_map/pallas_call | solution.py:581
  18.8 3.9 %collective-permute-done.5.refs_16_ = f32[6,8,128]{2,1,0:T(8,128)S(1)} collective-permute-done((f32[6,8,128]{2,1,0:T(8,128)S(1)}, f32[6,8,128]{2,1,0:T(8,128)S(1)}, u32[]{:S(2)}, u32[]{:S(2)}) %collective-permute-start.5) | collective-permute-done | bytes 24608 | tf_op jit(solution)/shard_map/ppermute | solution.py:603
  22.7 0.8 %shard_map.70 = (f32[5,256,128]{2,1,0:T(8,128)S(1)}, f32[5,8,128]{2,1,0:T(8,128)S(1)}, f32[5,8,128]{2,1,0:T(8,128)S(1)}, f32[5,8,128]{2,1,0:T(8,128)S(1)}, f32[5...) custom-call(s32[1]{0:T(128)} %bitcast.refs_0_, ...), custom_call_target="tpu_custom_call" | custom-call | flops 8000000 | bytes 4000000 | tf_op jit(solution)/shard_map/pallas_call | solution.py:581
  23.5 0.6 collective-permute-start.10
  24.1 3.1 %collective-permute-start.11 = (f32[5,8,128]{2,1,0:T(8,128)S(1)}, f32[5,8,128]{2,1,0:T(8,128)S(1)}, u32[]{:S(2)}, u32[]{:S(2)}) collective-permute-start(f32[5,8,128]{2,1,0:T(8,128)S(1)} %get-tuple-element.49.refs_10_), channel_id=1, source_target_pairs={{0,36},{1,37},{2,38},{3,39},{4,32},{5,33},{6,34},{7,35},{8,44},{9,... | collective-permute-start | bytes 61448 | tf_op jit(solution)/shard_map/ppermute | solution.py:603
  27.2 0.5 collective-permute-start.7
  27.8 0.6 %collective-permute-start.8 = (f32[5,8,128]{2,1,0:T(8,128)S(1)}, f32[5,8,128]{2,1,0:T(8,128)S(1)}, u32[]{:S(2)}, u32[]{:S(2)}) collective-permute-start(f32[5,8,128]{2,1,0:T(8,128)S(1)} %get-tuple-element.46.refs_7_), channel_id=1, source_target_pairs={{0,2},{1,3},{2,0},{3,1},{4,6},{5,7},{6,4},{7,5},{8,10},{9,11},{10,... | collective-permute-start | bytes 61448 | tf_op jit(solution)/shard_map/ppermute | solution.py:603
  28.3 0.5 collective-permute-done.10.refs_15_
  28.9 1.2 %collective-permute-start.9 = (f32[5,8,128]{2,1,0:T(8,128)S(1)}, f32[5,8,128]{2,1,0:T(8,128)S(1)}, u32[]{:S(2)}, u32[]{:S(2)}) collective-permute-start(f32[5,8,128]{2,1,0:T(8,128)S(1)} %get-tuple-element.47.refs_8_), channel_id=1, source_target_pairs={{0,18},{1,19},{2,16},{3,17},{4,22},{5,23},{6,20},{7,21},{8,26},{9,... | collective-permute-start | bytes 61448 | tf_op jit(solution)/shard_map/ppermute | solution.py:603
  30.1 1.3 %shard_map.71.refs_4_ = f32[6,256,128]{2,1,0:T(8,128)S(1)} custom-call(f32[5,256,128]{2,1,0:T(8,128)S(1)} %get-tuple-element.43.refs_0_, f32[256,128]{1,0:T(8,128)S(1)} %get-tuple-element.36.frac_ref.refs_1_.refs_2_), custom_call_target="tpu_custom_call" | custom-call | flops 8000000 | bytes 4000000 | tf_op jit(solution)/shard_map/pallas_call | solution.py:581
  31.4 1.5 %collective-permute-done.7.refs_12_ = f32[5,8,128]{2,1,0:T(8,128)S(1)} collective-permute-done((f32[5,8,128]{2,1,0:T(8,128)S(1)}, f32[5,8,128]{2,1,0:T(8,128)S(1)}, u32[]{:S(2)}, u32[]{:S(2)}) %collective-permute-start.7) | collective-permute-done | bytes 20512 | tf_op jit(solution)/shard_map/ppermute | solution.py:603
  33.0 2.1 %collective-permute-done.9.refs_14_ = f32[5,8,128]{2,1,0:T(8,128)S(1)} collective-permute-done((f32[5,8,128]{2,1,0:T(8,128)S(1)}, f32[5,8,128]{2,1,0:T(8,128)S(1)}, u32[]{:S(2)}, u32[]{:S(2)}) %collective-permute-start.9) | collective-permute-done | bytes 20512 | tf_op jit(solution)/shard_map/ppermute | solution.py:603
  35.1 0.8 %shard_map.72 = (f32[5,256,128]{2,1,0:T(8,128)S(1)}, f32[5,8,128]{2,1,0:T(8,128)S(1)}, f32[5,8,128]{2,1,0:T(8,128)S(1)}, f32[5,8,128]{2,1,0:T(8,128)S(1)}, f32[5...) custom-call(s32[1]{0:T(128)} %bitcast.refs_0_, ...), custom_call_target="tpu_custom_call" | custom-call | flops 8000000 | bytes 4000000 | tf_op jit(solution)/shard_map/pallas_call | solution.py:581
  36.0 2.6 %collective-permute-start.13 = (f32[5,8,128]{2,1,0:T(8,128)S(1)}, f32[5,8,128]{2,1,0:T(8,128)S(1)}, u32[]{:S(2)}, u32[]{:S(2)}) collective-permute-start(f32[5,8,128]{2,1,0:T(8,128)S(1)} %get-tuple-element.58.refs_6_), channel_id=1, source_target_pairs={{0,73},{1,8},{2,75},{3,10},{4,77},{5,12},{6,79},{7,14},{8,1},{9,64... | collective-permute-start | bytes 61448 | tf_op jit(solution)/shard_map/ppermute | solution.py:603
  38.5 1.4 %collective-permute-start.14 = (f32[5,8,128]{2,1,0:T(8,128)S(1)}, f32[5,8,128]{2,1,0:T(8,128)S(1)}, u32[]{:S(2)}, u32[]{:S(2)}) collective-permute-start(f32[5,8,128]{2,1,0:T(8,128)S(1)} %get-tuple-element.59.refs_7_), channel_id=1, source_target_pairs={{0,2},{1,3},{2,0},{3,1},{4,6},{5,7},{6,4},{7,5},{8,10},{9,11},{10,... | collective-permute-start | bytes 61448 | tf_op jit(solution)/shard_map/ppermute | solution.py:603
  40.0 1.0 %collective-permute-start.15 = (f32[5,8,128]{2,1,0:T(8,128)S(1)}, f32[5,8,128]{2,1,0:T(8,128)S(1)}, u32[]{:S(2)}, u32[]{:S(2)}) collective-permute-start(f32[5,8,128]{2,1,0:T(8,128)S(1)} %get-tuple-element.60.refs_8_), channel_id=1, source_target_pairs={{0,18},{1,19},{2,16},{3,17},{4,22},{5,23},{6,20},{7,21},{8,26},{9,... | collective-permute-start | bytes 61448 | tf_op jit(solution)/shard_map/ppermute | solution.py:603
  41.0 1.0 %collective-permute-start.16 = (f32[5,8,128]{2,1,0:T(8,128)S(1)}, f32[5,8,128]{2,1,0:T(8,128)S(1)}, u32[]{:S(2)}, u32[]{:S(2)}) collective-permute-start(f32[5,8,128]{2,1,0:T(8,128)S(1)} %get-tuple-element.61.refs_9_), channel_id=1, source_target_pairs={{0,4},{1,5},{2,6},{3,7},{4,0},{5,1},{6,2},{7,3},{8,12},{9,13},{10,... | collective-permute-start | bytes 61448 | tf_op jit(solution)/shard_map/ppermute | solution.py:603
  42.0 2.6 %collective-permute-start.17 = (f32[5,8,128]{2,1,0:T(8,128)S(1)}, f32[5,8,128]{2,1,0:T(8,128)S(1)}, u32[]{:S(2)}, u32[]{:S(2)}) collective-permute-start(f32[5,8,128]{2,1,0:T(8,128)S(1)} %get-tuple-element.62.refs_10_), channel_id=1, source_target_pairs={{0,36},{1,37},{2,38},{3,39},{4,32},{5,33},{6,34},{7,35},{8,44},{9,... | collective-permute-start | bytes 61448 | tf_op jit(solution)/shard_map/ppermute | solution.py:603
  44.6 0.2 shard_map.73
  44.9 1.2 %shard_map.76.refs_1_ = f32[5,256,128]{2,1,0:T(8,128)S(1)} custom-call(f32[5,256,128]{2,1,0:T(8,128)S(1)} %get-tuple-element.51.u_ref.refs_0_, f32[256,128]{1,0:T(8,128)S(1)} %get-tuple-element.36.frac_ref.refs_1_.refs_2_), custom_call_target="tpu_custom_call" | custom-call | flops 8000000 | bytes 4000000 | tf_op jit(solution)/shard_map/pallas_call | solution.py:581
  46.0 0.5 shard_map.75
  46.6 1.6 %collective-permute-done.17.refs_16_ = f32[5,8,128]{2,1,0:T(8,128)S(1)} collective-permute-done((f32[5,8,128]{2,1,0:T(8,128)S(1)}, f32[5,8,128]{2,1,0:T(8,128)S(1)}, u32[]{:S(2)}, u32[]{:S(2)}) %collective-permute-start.17) | collective-permute-done | bytes 20512 | tf_op jit(solution)/shard_map/ppermute | solution.py:603
  48.2 0.6 %shard_map.77 = (f32[5,4,512]{2,1,0:T(4,128)S(1)}, f32[11,4,512]{2,1,0:T(4,128)S(1)}) custom-call(s32[1]{0:T(128)} %bitcast.refs_0_, f32[5,256,128]{2,1,0:T(8,128)S(1)} %shard_map.76.refs_1_, f32[6,8,128]{2,1,0:T(8,128)S(1)} %get-tuple-element.50.refs_17_.refs_2_, f32[128,128]{1,0:T(8,128)S(1)} %get-tuple-element.54.order_ref.refs_3_, ...), custom_call_target="tpu_custom_call" | custom-call | flops 8000000 | bytes 4000000 | tf_op jit(solution)/shard_map/pallas_call | solution.py:581
  48.9 1.6 %shard_map.74 = f32[5,64,512]{2,1,0:T(8,128)} custom-call(f32[5,256,128]{2,1,0:T(8,128)S(1)} %get-tuple-element.51.u_ref.refs_0_, f32[2,64,128]{2,1,0:T(8,128)S(1)} %get-tuple-element.52.spread_ref), custom_call_target="tpu_custom_call" | custom-call | flops 8000000 | bytes 4000000 | tf_op jit(solution)/shard_map/pallas_call | solution.py:581
  50.5 7.8 %collective-permute-done.18.got_ref = f32[11,4,512]{2,1,0:T(4,128)S(1)} collective-permute-done((f32[11,4,512]{2,1,0:T(4,128)S(1)}, f32[11,4,512]{2,1,0:T(4,128)S(1)}, u32[]{:S(2)}, u32[]{:S(2)}) %collective-permute-start.18) | collective-permute-done | bytes 90144 | tf_op jit(solution)/shard_map/ppermute | solution.py:674
  58.2 0.8 %shard_map.78 = (f32[5,8,512]{2,1,0:T(8,128)}, f32[5,8,512]{2,1,0:T(8,128)}) custom-call(f32[8,128]{1,0:T(8,128)S(1)} %get-tuple-element.53.pick_ref, f32[6,4,512]{2,1,0:T(4,128)S(1)} %get-tuple-element.55.kept_state_ref, f32[5,4,512]{2,1,0:T(4,128)S(1)} %get-tuple-element.63.kept_res_ref, f32[11,4,512]{2,1,0:T(4,128)S(1)} %collective-permute-done.18.got_ref), custom_call_target="tpu_custom_call" | custom-call | flops 8000000 | bytes 4000000 | tf_op jit(solution)/shard_map/pallas_call | solution.py:581
  (22 shorter events, 0.6 us)
Async XLA Ops:
  3.5 12.9 %collective-permute-start = (f32[6,8,128]{2,1,0:T(8,128)S(1)}, f32[6,8,128]{2,1,0:T(8,128)S(1)}, u32[]{:S(2)}, u32[]{:S(2)}) collective-permute-start(f32[6,8,128]{2,1,0:T(8,128)S(1)} %get-tuple-element.37.refs_5_), channel_id=1, source_target_pairs={{0,1},{1,0},{2,3},{3,2},{4,5},{5,4},{6,7},{7,6},{8,9},{9,8},{10,11... | collective-permute-start | bytes 73736 | tf_op jit(solution)/shard_map/ppermute | solution.py:603
  3.6 14.9 %collective-permute-start.1 = (f32[6,8,128]{2,1,0:T(8,128)S(1)}, f32[6,8,128]{2,1,0:T(8,128)S(1)}, u32[]{:S(2)}, u32[]{:S(2)}) collective-permute-start(f32[6,8,128]{2,1,0:T(8,128)S(1)} %get-tuple-element.38.refs_6_), channel_id=1, source_target_pairs={{0,73},{1,8},{2,75},{3,10},{4,77},{5,12},{6,79},{7,14},{8,1},{9,64... | collective-permute-start | bytes 73736 | tf_op jit(solution)/shard_map/ppermute | solution.py:603
  8.4 10.1 %collective-permute-start.2 = (f32[6,8,128]{2,1,0:T(8,128)S(1)}, f32[6,8,128]{2,1,0:T(8,128)S(1)}, u32[]{:S(2)}, u32[]{:S(2)}) collective-permute-start(f32[6,8,128]{2,1,0:T(8,128)S(1)} %get-tuple-element.39.refs_7_), channel_id=1, source_target_pairs={{0,2},{1,3},{2,0},{3,1},{4,6},{5,7},{6,4},{7,5},{8,10},{9,11},{10,... | collective-permute-start | bytes 73736 | tf_op jit(solution)/shard_map/ppermute | solution.py:603
  9.9 8.7 %collective-permute-start.3 = (f32[6,8,128]{2,1,0:T(8,128)S(1)}, f32[6,8,128]{2,1,0:T(8,128)S(1)}, u32[]{:S(2)}, u32[]{:S(2)}) collective-permute-start(f32[6,8,128]{2,1,0:T(8,128)S(1)} %get-tuple-element.40.refs_8_), channel_id=1, source_target_pairs={{0,18},{1,19},{2,16},{3,17},{4,22},{5,23},{6,20},{7,21},{8,26},{9,... | collective-permute-start | bytes 73736 | tf_op jit(solution)/shard_map/ppermute | solution.py:603
  13.4 5.4 %collective-permute-start.4 = (f32[6,8,128]{2,1,0:T(8,128)S(1)}, f32[6,8,128]{2,1,0:T(8,128)S(1)}, u32[]{:S(2)}, u32[]{:S(2)}) collective-permute-start(f32[6,8,128]{2,1,0:T(8,128)S(1)} %get-tuple-element.41.refs_9_), channel_id=1, source_target_pairs={{0,4},{1,5},{2,6},{3,7},{4,0},{5,1},{6,2},{7,3},{8,12},{9,13},{10,... | collective-permute-start | bytes 73736 | tf_op jit(solution)/shard_map/ppermute | solution.py:603
  16.5 6.2 %collective-permute-start.5 = (f32[6,8,128]{2,1,0:T(8,128)S(1)}, f32[6,8,128]{2,1,0:T(8,128)S(1)}, u32[]{:S(2)}, u32[]{:S(2)}) collective-permute-start(f32[6,8,128]{2,1,0:T(8,128)S(1)} %get-tuple-element.42.refs_10_), channel_id=1, source_target_pairs={{0,36},{1,37},{2,38},{3,39},{4,32},{5,33},{6,34},{7,35},{8,44},{9,... | collective-permute-start | bytes 73736 | tf_op jit(solution)/shard_map/ppermute | solution.py:603
  23.5 5.4 %collective-permute-start.10 = (f32[5,8,128]{2,1,0:T(8,128)S(1)}, f32[5,8,128]{2,1,0:T(8,128)S(1)}, u32[]{:S(2)}, u32[]{:S(2)}) collective-permute-start(f32[5,8,128]{2,1,0:T(8,128)S(1)} %get-tuple-element.48.refs_9_), channel_id=1, source_target_pairs={{0,4},{1,5},{2,6},{3,7},{4,0},{5,1},{6,2},{7,3},{8,12},{9,13},{10,... | collective-permute-start | bytes 61448 | tf_op jit(solution)/shard_map/ppermute | solution.py:603
  24.1 7.3 %collective-permute-start.11 = (f32[5,8,128]{2,1,0:T(8,128)S(1)}, f32[5,8,128]{2,1,0:T(8,128)S(1)}, u32[]{:S(2)}, u32[]{:S(2)}) collective-permute-start(f32[5,8,128]{2,1,0:T(8,128)S(1)} %get-tuple-element.49.refs_10_), channel_id=1, source_target_pairs={{0,36},{1,37},{2,38},{3,39},{4,32},{5,33},{6,34},{7,35},{8,44},{9,... | collective-permute-start | bytes 61448 | tf_op jit(solution)/shard_map/ppermute | solution.py:603
  27.2 4.2 %collective-permute-start.6 = (f32[5,8,128]{2,1,0:T(8,128)S(1)}, f32[5,8,128]{2,1,0:T(8,128)S(1)}, u32[]{:S(2)}, u32[]{:S(2)}) collective-permute-start(f32[5,8,128]{2,1,0:T(8,128)S(1)} %get-tuple-element.44.refs_5_), channel_id=1, source_target_pairs={{0,1},{1,0},{2,3},{3,2},{4,5},{5,4},{6,7},{7,6},{8,9},{9,8},{10,11... | collective-permute-start | bytes 61448 | tf_op jit(solution)/shard_map/ppermute | solution.py:603
  27.2 5.7 %collective-permute-start.7 = (f32[5,8,128]{2,1,0:T(8,128)S(1)}, f32[5,8,128]{2,1,0:T(8,128)S(1)}, u32[]{:S(2)}, u32[]{:S(2)}) collective-permute-start(f32[5,8,128]{2,1,0:T(8,128)S(1)} %get-tuple-element.45.refs_6_), channel_id=1, source_target_pairs={{0,73},{1,8},{2,75},{3,10},{4,77},{5,12},{6,79},{7,14},{8,1},{9,64... | collective-permute-start | bytes 61448 | tf_op jit(solution)/shard_map/ppermute | solution.py:603
  27.8 5.2 %collective-permute-start.8 = (f32[5,8,128]{2,1,0:T(8,128)S(1)}, f32[5,8,128]{2,1,0:T(8,128)S(1)}, u32[]{:S(2)}, u32[]{:S(2)}) collective-permute-start(f32[5,8,128]{2,1,0:T(8,128)S(1)} %get-tuple-element.46.refs_7_), channel_id=1, source_target_pairs={{0,2},{1,3},{2,0},{3,1},{4,6},{5,7},{6,4},{7,5},{8,10},{9,11},{10,... | collective-permute-start | bytes 61448 | tf_op jit(solution)/shard_map/ppermute | solution.py:603
  28.9 6.2 %collective-permute-start.9 = (f32[5,8,128]{2,1,0:T(8,128)S(1)}, f32[5,8,128]{2,1,0:T(8,128)S(1)}, u32[]{:S(2)}, u32[]{:S(2)}) collective-permute-start(f32[5,8,128]{2,1,0:T(8,128)S(1)} %get-tuple-element.47.refs_8_), channel_id=1, source_target_pairs={{0,18},{1,19},{2,16},{3,17},{4,22},{5,23},{6,20},{7,21},{8,26},{9,... | collective-permute-start | bytes 61448 | tf_op jit(solution)/shard_map/ppermute | solution.py:603
  35.9 6.1 %collective-permute-start.12 = (f32[5,8,128]{2,1,0:T(8,128)S(1)}, f32[5,8,128]{2,1,0:T(8,128)S(1)}, u32[]{:S(2)}, u32[]{:S(2)}) collective-permute-start(f32[5,8,128]{2,1,0:T(8,128)S(1)} %get-tuple-element.57.refs_5_), channel_id=1, source_target_pairs={{0,1},{1,0},{2,3},{3,2},{4,5},{5,4},{6,7},{7,6},{8,9},{9,8},{10,11... | collective-permute-start | bytes 61448 | tf_op jit(solution)/shard_map/ppermute | solution.py:603
  36.0 8.7 %copy-start = (s32[64,6]{0,1:T(8,128)S(1)}, s32[64,6]{0,1:T(8,128)}, u32[]{:S(2)}) copy-start(s32[64,6]{0,1:T(8,128)} %param.6) | copy-start | bytes 4612
  36.0 10.6 %collective-permute-start.13 = (f32[5,8,128]{2,1,0:T(8,128)S(1)}, f32[5,8,128]{2,1,0:T(8,128)S(1)}, u32[]{:S(2)}, u32[]{:S(2)}) collective-permute-start(f32[5,8,128]{2,1,0:T(8,128)S(1)} %get-tuple-element.58.refs_6_), channel_id=1, source_target_pairs={{0,73},{1,8},{2,75},{3,10},{4,77},{5,12},{6,79},{7,14},{8,1},{9,64... | collective-permute-start | bytes 61448 | tf_op jit(solution)/shard_map/ppermute | solution.py:603
  38.5 8.0 %collective-permute-start.14 = (f32[5,8,128]{2,1,0:T(8,128)S(1)}, f32[5,8,128]{2,1,0:T(8,128)S(1)}, u32[]{:S(2)}, u32[]{:S(2)}) collective-permute-start(f32[5,8,128]{2,1,0:T(8,128)S(1)} %get-tuple-element.59.refs_7_), channel_id=1, source_target_pairs={{0,2},{1,3},{2,0},{3,1},{4,6},{5,7},{6,4},{7,5},{8,10},{9,11},{10,... | collective-permute-start | bytes 61448 | tf_op jit(solution)/shard_map/ppermute | solution.py:603
  40.0 6.6 %collective-permute-start.15 = (f32[5,8,128]{2,1,0:T(8,128)S(1)}, f32[5,8,128]{2,1,0:T(8,128)S(1)}, u32[]{:S(2)}, u32[]{:S(2)}) collective-permute-start(f32[5,8,128]{2,1,0:T(8,128)S(1)} %get-tuple-element.60.refs_8_), channel_id=1, source_target_pairs={{0,18},{1,19},{2,16},{3,17},{4,22},{5,23},{6,20},{7,21},{8,26},{9,... | collective-permute-start | bytes 61448 | tf_op jit(solution)/shard_map/ppermute | solution.py:603
  41.0 3.6 %copy-start.1 = (s32[64]{0:T(128)S(1)}, s32[64]{0:T(128)}, u32[]{:S(2)}) copy-start(s32[64]{0:T(128)} %param.7) | copy-start | bytes 772
  41.0 5.6 %collective-permute-start.16 = (f32[5,8,128]{2,1,0:T(8,128)S(1)}, f32[5,8,128]{2,1,0:T(8,128)S(1)}, u32[]{:S(2)}, u32[]{:S(2)}) collective-permute-start(f32[5,8,128]{2,1,0:T(8,128)S(1)} %get-tuple-element.61.refs_9_), channel_id=1, source_target_pairs={{0,4},{1,5},{2,6},{3,7},{4,0},{5,1},{6,2},{7,3},{8,12},{9,13},{10,... | collective-permute-start | bytes 61448 | tf_op jit(solution)/shard_map/ppermute | solution.py:603
  42.0 6.2 %collective-permute-start.17 = (f32[5,8,128]{2,1,0:T(8,128)S(1)}, f32[5,8,128]{2,1,0:T(8,128)S(1)}, u32[]{:S(2)}, u32[]{:S(2)}) collective-permute-start(f32[5,8,128]{2,1,0:T(8,128)S(1)} %get-tuple-element.62.refs_10_), channel_id=1, source_target_pairs={{0,36},{1,37},{2,38},{3,39},{4,32},{5,33},{6,34},{7,35},{8,44},{9,... | collective-permute-start | bytes 61448 | tf_op jit(solution)/shard_map/ppermute | solution.py:603
  48.8 9.5 %collective-permute-start.18 = (f32[11,4,512]{2,1,0:T(4,128)S(1)}, f32[11,4,512]{2,1,0:T(4,128)S(1)}, u32[]{:S(2)}, u32[]{:S(2)}) collective-permute-start(f32[11,4,512]{2,1,0:T(4,128)S(1)} %get-tuple-element.64), channel_id=1, source_target_pairs={{0,1},{1,2},{2,3},{3,4},{4,5},{5,6},{6,7},{7,8},{8,9},{9,10},{10,1... | collective-permute-start | bytes 270344 | tf_op jit(solution)/shard_map/ppermute | solution.py:674

commit v2 on v1

--- a/solution.py
+++ b/solution.py
@@ -39,14 +39,18 @@
             for device in range(count):
                 place = coordinates(device, count)
                 step = 1 if place[direction] % 2 == other else -1
-                place[direction] = (place[direction] + step) % extents[direction]
+                there = place[direction] + step
+                if direction == 1 or 0 <= there < extents[direction]:
+                    place[direction] = there % extents[direction]
+                else:
+                    place[1 if direction == 0 else 0] ^= 1
                 pairs.append((device, number[tuple(place)]))
             swaps.append(pairs)
     return swaps
 
 
-def cube_place(device_ref, count):
-    device = device_ref[0]
+def cube_place(count):
+    device = lax.axis_index(AXIS)
     place = coordinates(device, count)
     even = [place[direction] % 2 == 0 for direction in range(3)]
     far = [None, None, None]
@@ -333,7 +337,7 @@
     return place[1] * 32 + place[2] * 8 + place[0] * 2
 
 
-def prepare_kernel(count, device_ref, state_hbm, volume_hbm, neighbour_hbm, parent_hbm, *refs):
+def prepare_kernel(count, state_hbm, volume_hbm, neighbour_hbm, parent_hbm, *refs):
     u_ref, frac_ref = refs[0:2]
     message_refs = refs[2:8]
     state_ref, volume_ref, neighbour_ref, parent_ref, sems = refs[8:13]
@@ -346,7 +350,7 @@
         copies.append(pltpu.make_async_copy(state_hbm.at[q], state_ref.at[q], sems.at[3 + q]))
     for copy in copies:
         copy.start()
-    device, even, _ = cube_place(device_ref, count)
+    device, even, _ = cube_place(count)
     copies[0].wait()
     copies[1].wait()
     lane = as_column(brick_lane(device, neighbour_ref[...], parent_ref[...]), 64)
@@ -369,8 +373,8 @@
     write_messages([(u_ref, (q,)) for q in range(5)] + [(frac_ref, ())], message_refs, even)
 
 
-def tables_kernel(device_ref, neighbour_ref, parent_ref, spread_ref, order_ref, pick_ref):
-    device = device_ref[0]
+def tables_kernel(neighbour_ref, parent_ref, spread_ref, order_ref, pick_ref):
+    device = lax.axis_index(AXIS)
     parent_column = as_column(parent_ref[...], 64)
     lane = as_column(brick_lane(device, neighbour_ref[...], parent_ref[...]), 64)
     lanes = lane_index((64, LANES))
@@ -413,7 +417,7 @@
     interior_body(u_ref, frac_ref, res_ref, prim_ref, wx_ref, with_speed)
 
 
-def update_kernel(count, first, device_ref, *refs):
+def update_kernel(count, first, *refs):
     base_ref, frac_ref, mix_ref, inner_ref = refs[0:4]
     own_refs, ghost_refs = refs[4:10], refs[10:16]
     refs = refs[16:]
@@ -421,7 +425,7 @@
         new_ref, message_refs, faces_ref, res_ref = refs[0], refs[1:7], refs[7], refs[8]
     else:
         faces_ref, new_ref, message_refs, res_ref = refs[0], refs[1], refs[2:8], refs[8]
-    _, even, far = cube_place(device_ref, count)
+    _, even, far = cube_place(count)
     res_ref[...] = inner_ref[...]
 
     def aperture_of(direction, other):
@@ -518,11 +522,11 @@
             )
 
 
-def residual_kernel(count, device_ref, *refs):
+def residual_kernel(count, *refs):
     inner_ref, faces_ref, order_ref, sent_state_ref = refs[0:4]
     own_refs, ghost_refs = refs[4:10], refs[10:16]
     kept_ref, sent_ref, res_ref, rows_ref, half_ref = refs[16:21]
-    _, even, far = cube_place(device_ref, count)
+    _, even, far = cube_place(count)
     res_ref[...] = inner_ref[...]
     boundary_body(
         res_ref,
@@ -570,14 +574,10 @@
     return pltpu.VMEM(shape, F32)
 
 
-def call(kernel, outs, scratch, args, smem=1, sources=0):
+def call(kernel, outs, scratch, args, sources=0):
     vmem = pl.BlockSpec(memory_space=pltpu.VMEM)
-    spaces = [pltpu.SMEM] * smem + [pltpu.HBM] * sources
-    spaces += [pltpu.VMEM] * (len(args) - len(spaces))
-    args = [
-        pltpu.with_memory_space_constraint(arg, space) if space is not pltpu.SMEM else arg
-        for arg, space in zip(args, spaces)
-    ]
+    spaces = [pltpu.HBM] * sources + [pltpu.VMEM] * (len(args) - sources)
+    args = [pltpu.with_memory_space_constraint(arg, space) for arg, space in zip(args, spaces)]
     return pl.pallas_call(
         kernel,
         out_shape=outs,
@@ -589,7 +589,7 @@
     )(*args)
 
 
-START_ORDER = (5, 3, 1, 4, 2, 0)
+START_ORDER = (3, 1, 4, 5, 2, 0)
 
 
 def solution(mesh):
@@ -610,11 +610,9 @@
             [held(rows, ROWS, LANES)],
             [(5, ROWS, LANES), (rows, 64, LANES)],
             [u, frac],
-            0,
         )[0]
 
     def local(state, volume, neighbour, parent):
-        device = lax.axis_index(AXIS).astype(I32).reshape(1)
         parent = parent.reshape(1, 64)
         neighbour = neighbour.T
         grid = held(5, ROWS, LANES)
@@ -628,24 +626,23 @@
                 pltpu.VMEM((1, 64), I32),
                 pltpu.SemaphoreType.DMA((8,)),
             ],
-            [device, state, volume, neighbour, parent],
-            1,
+            [state, volume, neighbour, parent],
             4,
         )
         ghosts = exchange(sent)
         spread, order, pick = call(
-            lambda *refs: tables_kernel(*refs),
+            tables_kernel,
             [held(2, 64, LANES), held(LANES, LANES), held(8, LANES)],
             [],
-            [device, neighbour, parent],
-        )
-        mix = call(mixing_kernel, [held(ROWS, LANES)], [], [frac], 0)[0]
+            [neighbour, parent],
+        )
+        mix = call(mixing_kernel, [held(ROWS, LANES)], [], [frac])[0]
         inner = interior(u, frac, True)
         middle, *rest = call(
             lambda *refs: update_kernel(count, True, *refs),
             [grid] + [held(5, 8, LANES)] * 6 + [held(6, 8, LANES)],
             [(6, ROWS, LANES)],
-            [device, u, frac, mix, inner, *sent, *ghosts],
+            [u, frac, mix, inner, *sent, *ghosts],
         )
         sent, faces = rest[0:6], rest[6]
         ghosts = exchange(sent)
@@ -654,7 +651,7 @@
             lambda *refs: update_kernel(count, False, *refs),
             [grid] + [held(5, 8, LANES)] * 6,
             [(6, ROWS, LANES)],
-            [device, u, frac, mix, inner, *sent, *ghosts, faces],
+            [u, frac, mix, inner, *sent, *ghosts, faces],
         )
         ghosts = exchange(sent)
         inner = interior(fine, frac, False)
@@ -663,22 +660,17 @@
             [held(6, 4, 512), held(6, 4, 512)],
             [(LANES, LANES), (64, LANES)],
             [fine, frac, order],
-            0,
         )
         kept_res, outgoing = call(
             lambda *refs: residual_kernel(count, *refs),
             [held(5, 4, 512), held(11, 4, 512)],
             [(5, ROWS, LANES), (LANES, LANES), (64, LANES)],
-            [device, inner, faces, order, sent_state, *sent, *ghosts],
+            [inner, faces, order, sent_state, *sent, *ghosts],
         )
         got = lax.ppermute(outgoing, AXIS, forward)
-        fine_out = call(output_kernel, [f32(5, 64, 512)], [], [fine, spread], 0)[0]
+        fine_out = call(output_kernel, [f32(5, 64, 512)], [], [fine, spread])[0]
         coarse_state, coarse_residual = call(
-            coarse_kernel,
-            [f32(5, 8, 512), f32(5, 8, 512)],
-            [],
-            [pick, kept_state, kept_res, got],
-            0,
+            coarse_kernel, [f32(5, 8, 512), f32(5, 8, 512)], [], [pick, kept_state, kept_res, got]
         )
         return fine_out, coarse_state, coarse_residual
 

time: 59.1 us -> 54.5 us (0.922)
  the two profiles are of different devices: /device:TPU:0 before, /device:TPU:24 now
where the time goes in v2:
time: 54.5 us; the launch traced here: 54.4 us
  waiting for transfers between devices  23.1 us (42%)
  starting transfers between devices  18.4 us (34%)
  Pallas kernels  12 us (22%)
  between operations  0.81 us (1%)
    ppermute x18, starting transfers between devices, exchange(): ghosts[number] = lax.ppermute(messages[number], AXIS, swaps[number])  18.3 us
    ppermute x18, waiting for transfers between devices, exchange(): ghosts[number] = lax.ppermute(messages[number], AXIS, swaps[number])  16.6 us
    pallas_call x12, Pallas kernels, call(): pl.pallas_call(kernel, out_shape=outs, in_specs=[pl.BlockSpec(memory_spac...  12 us
    ppermute x1, waiting for transfers between devices, local(): got = lax.ppermute(outgoing, AXIS, forward)  6.57 us
  transfers between devices with their start and end apart: 19, of which 7 were waited for; matrix products, arithmetic and copies ran while one was open for 0% of the time, Pallas kernels for 11%

profile of v2, /device:TPU:24, one launch (start us, length us, event | category | flops | bytes accessed | tf_op | source)
XLA Modules:
  0.0 54.4 jit_solution(4214347914376960650)
XLA Ops:
  0.6 2.9 %shard_map.67 = (f32[5,256,128]{2,1,0:T(8,128)S(1)}, f32[256,128]{1,0:T(8,128)S(1)}, f32[6,8,128]{2,1,0:T(8,128)S(1)}, f32[6,8,128]{2,1,0:T(8,128)S(1)}, f32[6,8...) custom-call(f32[5,64,512]{2,1,0:T(8,128)} %refs_0_.1, ...), custom_call_target="tpu_custom_call" | custom-call | flops 8000000 | bytes 4000000 | tf_op jit(solution)/shard_map/pallas_call | solution.py:581
  3.6 2.7 %collective-permute-start.1 = (f32[6,8,128]{2,1,0:T(8,128)S(1)}, f32[6,8,128]{2,1,0:T(8,128)S(1)}, u32[]{:S(2)}, u32[]{:S(2)}) collective-permute-start(f32[6,8,128]{2,1,0:T(8,128)S(1)} %get-tuple-element.38.refs_5_), channel_id=1, source_target_pairs={{0,2},{1,8},{2,0},{3,10},{4,6},{5,12},{6,4},{7,14},{8,1},{9,64},{1... | collective-permute-start | bytes 73736 | tf_op jit(solution)/shard_map/ppermute | solution.py:603
  6.3 1.5 %collective-permute-start.2 = (f32[6,8,128]{2,1,0:T(8,128)S(1)}, f32[6,8,128]{2,1,0:T(8,128)S(1)}, u32[]{:S(2)}, u32[]{:S(2)}) collective-permute-start(f32[6,8,128]{2,1,0:T(8,128)S(1)} %get-tuple-element.39.refs_6_), channel_id=1, source_target_pairs={{0,2},{1,3},{2,0},{3,1},{4,6},{5,7},{6,4},{7,5},{8,10},{9,11},{10,... | collective-permute-start | bytes 73736 | tf_op jit(solution)/shard_map/ppermute | solution.py:603
  7.8 3.6 %collective-permute-start.3 = (f32[6,8,128]{2,1,0:T(8,128)S(1)}, f32[6,8,128]{2,1,0:T(8,128)S(1)}, u32[]{:S(2)}, u32[]{:S(2)}) collective-permute-start(f32[6,8,128]{2,1,0:T(8,128)S(1)} %get-tuple-element.40.refs_7_), channel_id=1, source_target_pairs={{0,18},{1,19},{2,16},{3,17},{4,22},{5,23},{6,20},{7,21},{8,26},{9,... | collective-permute-start | bytes 73736 | tf_op jit(solution)/shard_map/ppermute | solution.py:603
  11.4 3.0 %collective-permute-start.4 = (f32[6,8,128]{2,1,0:T(8,128)S(1)}, f32[6,8,128]{2,1,0:T(8,128)S(1)}, u32[]{:S(2)}, u32[]{:S(2)}) collective-permute-start(f32[6,8,128]{2,1,0:T(8,128)S(1)} %get-tuple-element.41.refs_8_), channel_id=1, source_target_pairs={{0,4},{1,5},{2,6},{3,7},{4,0},{5,1},{6,2},{7,3},{8,12},{9,13},{10,... | collective-permute-start | bytes 73736 | tf_op jit(solution)/shard_map/ppermute | solution.py:603
  14.4 0.1 shard_map.68.refs_2_
  14.5 1.3 %shard_map.69.refs_3_ = f32[6,256,128]{2,1,0:T(8,128)S(1)} custom-call(f32[5,256,128]{2,1,0:T(8,128)S(1)} %get-tuple-element.35.refs_0_, f32[256,128]{1,0:T(8,128)S(1)} %get-tuple-element.36.frac_ref.refs_1_), custom_call_target="tpu_custom_call" | custom-call | flops 8000000 | bytes 4000000 | tf_op jit(solution)/shard_map/pallas_call | solution.py:581
  15.8 0.9 %collective-permute-done.4.refs_14_ = f32[6,8,128]{2,1,0:T(8,128)S(1)} collective-permute-done((f32[6,8,128]{2,1,0:T(8,128)S(1)}, f32[6,8,128]{2,1,0:T(8,128)S(1)}, u32[]{:S(2)}, u32[]{:S(2)}) %collective-permute-start.4) | collective-permute-done | bytes 24608 | tf_op jit(solution)/shard_map/ppermute | solution.py:603
  16.7 3.9 %collective-permute-done.5.refs_15_ = f32[6,8,128]{2,1,0:T(8,128)S(1)} collective-permute-done((f32[6,8,128]{2,1,0:T(8,128)S(1)}, f32[6,8,128]{2,1,0:T(8,128)S(1)}, u32[]{:S(2)}, u32[]{:S(2)}) %collective-permute-start.5) | collective-permute-done | bytes 24608 | tf_op jit(solution)/shard_map/ppermute | solution.py:603
  20.6 0.8 %shard_map.70 = (f32[5,256,128]{2,1,0:T(8,128)S(1)}, f32[5,8,128]{2,1,0:T(8,128)S(1)}, f32[5,8,128]{2,1,0:T(8,128)S(1)}, f32[5,8,128]{2,1,0:T(8,128)S(1)}, f32[5...) custom-call(f32[5,256,128]{2,1,0:T(8,128)S(1)} %get-tuple-element.35.refs_0, ...), custom_call_target="tpu_custom_call" | custom-call | flops 8000000 | bytes 4000000 | tf_op jit(solution)/shard_map/pallas_call | solution.py:581
  21.4 0.1 collective-permute-start.10
  21.5 0.3 collective-permute-start.11
  21.8 0.2 collective-permute-start.7
  22.1 1.3 %collective-permute-start.8 = (f32[5,8,128]{2,1,0:T(8,128)S(1)}, f32[5,8,128]{2,1,0:T(8,128)S(1)}, u32[]{:S(2)}, u32[]{:S(2)}) collective-permute-start(f32[5,8,128]{2,1,0:T(8,128)S(1)} %get-tuple-element.46.refs_6_), channel_id=1, source_target_pairs={{0,2},{1,3},{2,0},{3,1},{4,6},{5,7},{6,4},{7,5},{8,10},{9,11},{10,... | collective-permute-start | bytes 61448 | tf_op jit(solution)/shard_map/ppermute | solution.py:603
  23.4 3.4 %collective-permute-done.10.refs_14_ = f32[5,8,128]{2,1,0:T(8,128)S(1)} collective-permute-done((f32[5,8,128]{2,1,0:T(8,128)S(1)}, f32[5,8,128]{2,1,0:T(8,128)S(1)}, u32[]{:S(2)}, u32[]{:S(2)}) %collective-permute-start.10) | collective-permute-done | bytes 20512 | tf_op jit(solution)/shard_map/ppermute | solution.py:603
  26.8 1.3 %shard_map.71.refs_3_ = f32[6,256,128]{2,1,0:T(8,128)S(1)} custom-call(f32[5,256,128]{2,1,0:T(8,128)S(1)} %get-tuple-element.43.refs_0_, f32[256,128]{1,0:T(8,128)S(1)} %get-tuple-element.36.frac_ref.refs_1_), custom_call_target="tpu_custom_call" | custom-call | flops 8000000 | bytes 4000000 | tf_op jit(solution)/shard_map/pallas_call | solution.py:581
  28.1 4.8 %collective-permute-done.9.refs_13_ = f32[5,8,128]{2,1,0:T(8,128)S(1)} collective-permute-done((f32[5,8,128]{2,1,0:T(8,128)S(1)}, f32[5,8,128]{2,1,0:T(8,128)S(1)}, u32[]{:S(2)}, u32[]{:S(2)}) %collective-permute-start.9) | collective-permute-done | bytes 20512 | tf_op jit(solution)/shard_map/ppermute | solution.py:603
  33.0 0.8 %shard_map.72 = (f32[5,256,128]{2,1,0:T(8,128)S(1)}, f32[5,8,128]{2,1,0:T(8,128)S(1)}, f32[5,8,128]{2,1,0:T(8,128)S(1)}, f32[5,8,128]{2,1,0:T(8,128)S(1)}, f32[5...) custom-call(f32[5,256,128]{2,1,0:T(8,128)S(1)} %get-tuple-element.35.refs_0_, ...), custom_call_target="tpu_custom_call" | custom-call | flops 8000000 | bytes 4000000 | tf_op jit(solution)/shard_map/pallas_call | solution.py:581
  33.8 0.1 collective-permute-start.13
  34.0 0.6 %collective-permute-start.14 = (f32[5,8,128]{2,1,0:T(8,128)S(1)}, f32[5,8,128]{2,1,0:T(8,128)S(1)}, u32[]{:S(2)}, u32[]{:S(2)}) collective-permute-start(f32[5,8,128]{2,1,0:T(8,128)S(1)} %get-tuple-element.59.refs_6_), channel_id=1, source_target_pairs={{0,2},{1,3},{2,0},{3,1},{4,6},{5,7},{6,4},{7,5},{8,10},{9,11},{10,... | collective-permute-start | bytes 61448 | tf_op jit(solution)/shard_map/ppermute | solution.py:603
  34.6 1.7 %collective-permute-start.15 = (f32[5,8,128]{2,1,0:T(8,128)S(1)}, f32[5,8,128]{2,1,0:T(8,128)S(1)}, u32[]{:S(2)}, u32[]{:S(2)}) collective-permute-start(f32[5,8,128]{2,1,0:T(8,128)S(1)} %get-tuple-element.60.refs_7_), channel_id=1, source_target_pairs={{0,18},{1,19},{2,16},{3,17},{4,22},{5,23},{6,20},{7,21},{8,26},{9,... | collective-permute-start | bytes 61448 | tf_op jit(solution)/shard_map/ppermute | solution.py:603
  36.3 2.2 %collective-permute-start.16 = (f32[5,8,128]{2,1,0:T(8,128)S(1)}, f32[5,8,128]{2,1,0:T(8,128)S(1)}, u32[]{:S(2)}, u32[]{:S(2)}) collective-permute-start(f32[5,8,128]{2,1,0:T(8,128)S(1)} %get-tuple-element.61.refs_8_), channel_id=1, source_target_pairs={{0,4},{1,5},{2,6},{3,7},{4,0},{5,1},{6,2},{7,3},{8,12},{9,13},{10,... | collective-permute-start | bytes 61448 | tf_op jit(solution)/shard_map/ppermute | solution.py:603
  38.5 0.7 %collective-permute-start.17 = (f32[5,8,128]{2,1,0:T(8,128)S(1)}, f32[5,8,128]{2,1,0:T(8,128)S(1)}, u32[]{:S(2)}, u32[]{:S(2)}) collective-permute-start(f32[5,8,128]{2,1,0:T(8,128)S(1)} %get-tuple-element.62.refs_9_), channel_id=1, source_target_pairs={{0,1},{1,0},{2,3},{3,2},{4,32},{5,33},{6,34},{7,35},{8,9},{9,8},{1... | collective-permute-start | bytes 61448 | tf_op jit(solution)/shard_map/ppermute | solution.py:603
  39.3 0.2 shard_map.73
  39.5 1.1 %shard_map.76.refs_0_ = f32[5,256,128]{2,1,0:T(8,128)S(1)} custom-call(f32[5,256,128]{2,1,0:T(8,128)S(1)} %get-tuple-element.51.u_ref.refs_0_, f32[256,128]{1,0:T(8,128)S(1)} %get-tuple-element.36.frac_ref.refs_1_), custom_call_target="tpu_custom_call" | custom-call | flops 8000000 | bytes 4000000 | tf_op jit(solution)/shard_map/pallas_call | solution.py:581
  40.7 0.5 shard_map.75
  41.2 0.4 collective-permute-done.16.refs_14_
  41.6 3.1 %collective-permute-done.17.refs_15_ = f32[5,8,128]{2,1,0:T(8,128)S(1)} collective-permute-done((f32[5,8,128]{2,1,0:T(8,128)S(1)}, f32[5,8,128]{2,1,0:T(8,128)S(1)}, u32[]{:S(2)}, u32[]{:S(2)}) %collective-permute-start.17) | collective-permute-done | bytes 20512 | tf_op jit(solution)/shard_map/ppermute | solution.py:603
  44.7 0.7 %shard_map.77 = (f32[5,4,512]{2,1,0:T(4,128)S(1)}, f32[11,4,512]{2,1,0:T(4,128)S(1)}) custom-call(f32[5,256,128]{2,1,0:T(8,128)S(1)} %shard_map.76.refs_0_, f32[6,8,128]{2,1,0:T(8,128)S(1)} %get-tuple-element.50.refs_16_.refs_1_, f32[128,128]{1,0:T(8,128)S(1)} %get-tuple-element.54.order_ref.refs_2_, f32[6,4,512]{2,1,0:T(4,128)S(1)} %get-tuple-element.56.refs_3_, ...), custom_call_target="tpu_custom_call" | custom-call | flops 8000000 | bytes 4000000 | tf_op jit(solution)/shard_map/pallas_call | solution.py:581
  45.5 1.6 %shard_map.74 = f32[5,64,512]{2,1,0:T(8,128)} custom-call(f32[5,256,128]{2,1,0:T(8,128)S(1)} %get-tuple-element.51.u_ref.refs_0_, f32[2,64,128]{2,1,0:T(8,128)S(1)} %get-tuple-element.52.spread_ref), custom_call_target="tpu_custom_call" | custom-call | flops 8000000 | bytes 4000000 | tf_op jit(solution)/shard_map/pallas_call | solution.py:581
  47.0 6.6 %collective-permute-done.18.got_ref = f32[11,4,512]{2,1,0:T(4,128)S(1)} collective-permute-done((f32[11,4,512]{2,1,0:T(4,128)S(1)}, f32[11,4,512]{2,1,0:T(4,128)S(1)}, u32[]{:S(2)}, u32[]{:S(2)}) %collective-permute-start.18) | collective-permute-done | bytes 90144 | tf_op jit(solution)/shard_map/ppermute | solution.py:670
  53.6 0.8 %shard_map.78 = (f32[5,8,512]{2,1,0:T(8,128)}, f32[5,8,512]{2,1,0:T(8,128)}) custom-call(f32[8,128]{1,0:T(8,128)S(1)} %get-tuple-element.53.pick_ref, f32[6,4,512]{2,1,0:T(4,128)S(1)} %get-tuple-element.55.kept_state_ref, f32[5,4,512]{2,1,0:T(4,128)S(1)} %get-tuple-element.63.kept_res_ref, f32[11,4,512]{2,1,0:T(4,128)S(1)} %collective-permute-done.18.got_ref), custom_call_target="tpu_custom_call" | custom-call | flops 8000000 | bytes 4000000 | tf_op jit(solution)/shard_map/pallas_call | solution.py:581
  (22 shorter events, 0.3 us)
Async XLA Ops:
  3.5 10.9 %collective-permute-start = (f32[6,8,128]{2,1,0:T(8,128)S(1)}, f32[6,8,128]{2,1,0:T(8,128)S(1)}, u32[]{:S(2)}, u32[]{:S(2)}) collective-permute-start(f32[6,8,128]{2,1,0:T(8,128)S(1)} %get-tuple-element.37.refs_4_), channel_id=1, source_target_pairs={{0,1},{1,0},{2,3},{3,2},{4,5},{5,4},{6,7},{7,6},{8,9},{9,8},{10,11... | collective-permute-start | bytes 73736 | tf_op jit(solution)/shard_map/ppermute | solution.py:603
  3.6 12.2 %collective-permute-start.1 = (f32[6,8,128]{2,1,0:T(8,128)S(1)}, f32[6,8,128]{2,1,0:T(8,128)S(1)}, u32[]{:S(2)}, u32[]{:S(2)}) collective-permute-start(f32[6,8,128]{2,1,0:T(8,128)S(1)} %get-tuple-element.38.refs_5_), channel_id=1, source_target_pairs={{0,2},{1,8},{2,0},{3,10},{4,6},{5,12},{6,4},{7,14},{8,1},{9,64},{1... | collective-permute-start | bytes 73736 | tf_op jit(solution)/shard_map/ppermute | solution.py:603
  6.3 9.5 %collective-permute-start.2 = (f32[6,8,128]{2,1,0:T(8,128)S(1)}, f32[6,8,128]{2,1,0:T(8,128)S(1)}, u32[]{:S(2)}, u32[]{:S(2)}) collective-permute-start(f32[6,8,128]{2,1,0:T(8,128)S(1)} %get-tuple-element.39.refs_6_), channel_id=1, source_target_pairs={{0,2},{1,3},{2,0},{3,1},{4,6},{5,7},{6,4},{7,5},{8,10},{9,11},{10,... | collective-permute-start | bytes 73736 | tf_op jit(solution)/shard_map/ppermute | solution.py:603
  7.8 8.0 %collective-permute-start.3 = (f32[6,8,128]{2,1,0:T(8,128)S(1)}, f32[6,8,128]{2,1,0:T(8,128)S(1)}, u32[]{:S(2)}, u32[]{:S(2)}) collective-permute-start(f32[6,8,128]{2,1,0:T(8,128)S(1)} %get-tuple-element.40.refs_7_), channel_id=1, source_target_pairs={{0,18},{1,19},{2,16},{3,17},{4,22},{5,23},{6,20},{7,21},{8,26},{9,... | collective-permute-start | bytes 73736 | tf_op jit(solution)/shard_map/ppermute | solution.py:603
  11.4 5.3 %collective-permute-start.4 = (f32[6,8,128]{2,1,0:T(8,128)S(1)}, f32[6,8,128]{2,1,0:T(8,128)S(1)}, u32[]{:S(2)}, u32[]{:S(2)}) collective-permute-start(f32[6,8,128]{2,1,0:T(8,128)S(1)} %get-tuple-element.41.refs_8_), channel_id=1, source_target_pairs={{0,4},{1,5},{2,6},{3,7},{4,0},{5,1},{6,2},{7,3},{8,12},{9,13},{10,... | collective-permute-start | bytes 73736 | tf_op jit(solution)/shard_map/ppermute | solution.py:603
  14.4 6.2 %collective-permute-start.5 = (f32[6,8,128]{2,1,0:T(8,128)S(1)}, f32[6,8,128]{2,1,0:T(8,128)S(1)}, u32[]{:S(2)}, u32[]{:S(2)}) collective-permute-start(f32[6,8,128]{2,1,0:T(8,128)S(1)} %get-tuple-element.42.refs_9_), channel_id=1, source_target_pairs={{0,1},{1,0},{2,3},{3,2},{4,32},{5,33},{6,34},{7,35},{8,9},{9,8},{1... | collective-permute-start | bytes 73736 | tf_op jit(solution)/shard_map/ppermute | solution.py:603
  21.4 5.4 %collective-permute-start.10 = (f32[5,8,128]{2,1,0:T(8,128)S(1)}, f32[5,8,128]{2,1,0:T(8,128)S(1)}, u32[]{:S(2)}, u32[]{:S(2)}) collective-permute-start(f32[5,8,128]{2,1,0:T(8,128)S(1)} %get-tuple-element.48.refs_8_), channel_id=1, source_target_pairs={{0,4},{1,5},{2,6},{3,7},{4,0},{5,1},{6,2},{7,3},{8,12},{9,13},{10,... | collective-permute-start | bytes 61448 | tf_op jit(solution)/shard_map/ppermute | solution.py:603
  21.5 6.6 %collective-permute-start.11 = (f32[5,8,128]{2,1,0:T(8,128)S(1)}, f32[5,8,128]{2,1,0:T(8,128)S(1)}, u32[]{:S(2)}, u32[]{:S(2)}) collective-permute-start(f32[5,8,128]{2,1,0:T(8,128)S(1)} %get-tuple-element.49.refs_9_), channel_id=1, source_target_pairs={{0,1},{1,0},{2,3},{3,2},{4,32},{5,33},{6,34},{7,35},{8,9},{9,8},{1... | collective-permute-start | bytes 61448 | tf_op jit(solution)/shard_map/ppermute | solution.py:603
  21.8 6.2 %collective-permute-start.6 = (f32[5,8,128]{2,1,0:T(8,128)S(1)}, f32[5,8,128]{2,1,0:T(8,128)S(1)}, u32[]{:S(2)}, u32[]{:S(2)}) collective-permute-start(f32[5,8,128]{2,1,0:T(8,128)S(1)} %get-tuple-element.44.refs_4_), channel_id=1, source_target_pairs={{0,1},{1,0},{2,3},{3,2},{4,5},{5,4},{6,7},{7,6},{8,9},{9,8},{10,11... | collective-permute-start | bytes 61448 | tf_op jit(solution)/shard_map/ppermute | solution.py:603
  21.8 6.3 %collective-permute-start.7 = (f32[5,8,128]{2,1,0:T(8,128)S(1)}, f32[5,8,128]{2,1,0:T(8,128)S(1)}, u32[]{:S(2)}, u32[]{:S(2)}) collective-permute-start(f32[5,8,128]{2,1,0:T(8,128)S(1)} %get-tuple-element.45.refs_5_), channel_id=1, source_target_pairs={{0,2},{1,8},{2,0},{3,10},{4,6},{5,12},{6,4},{7,14},{8,1},{9,64},{1... | collective-permute-start | bytes 61448 | tf_op jit(solution)/shard_map/ppermute | solution.py:603
  22.1 6.1 %collective-permute-start.8 = (f32[5,8,128]{2,1,0:T(8,128)S(1)}, f32[5,8,128]{2,1,0:T(8,128)S(1)}, u32[]{:S(2)}, u32[]{:S(2)}) collective-permute-start(f32[5,8,128]{2,1,0:T(8,128)S(1)} %get-tuple-element.46.refs_6_), channel_id=1, source_target_pairs={{0,2},{1,3},{2,0},{3,1},{4,6},{5,7},{6,4},{7,5},{8,10},{9,11},{10,... | collective-permute-start | bytes 61448 | tf_op jit(solution)/shard_map/ppermute | solution.py:603
  26.8 6.2 %collective-permute-start.9 = (f32[5,8,128]{2,1,0:T(8,128)S(1)}, f32[5,8,128]{2,1,0:T(8,128)S(1)}, u32[]{:S(2)}, u32[]{:S(2)}) collective-permute-start(f32[5,8,128]{2,1,0:T(8,128)S(1)} %get-tuple-element.47.refs_7_), channel_id=1, source_target_pairs={{0,18},{1,19},{2,16},{3,17},{4,22},{5,23},{6,20},{7,21},{8,26},{9,... | collective-permute-start | bytes 61448 | tf_op jit(solution)/shard_map/ppermute | solution.py:603
  33.7 4.8 %collective-permute-start.12 = (f32[5,8,128]{2,1,0:T(8,128)S(1)}, f32[5,8,128]{2,1,0:T(8,128)S(1)}, u32[]{:S(2)}, u32[]{:S(2)}) collective-permute-start(f32[5,8,128]{2,1,0:T(8,128)S(1)} %get-tuple-element.57.refs_4_), channel_id=1, source_target_pairs={{0,1},{1,0},{2,3},{3,2},{4,5},{5,4},{6,7},{7,6},{8,9},{9,8},{10,11... | collective-permute-start | bytes 61448 | tf_op jit(solution)/shard_map/ppermute | solution.py:603
  33.8 5.5 %copy-start = (s32[64,6]{0,1:T(8,128)S(1)}, s32[64,6]{0,1:T(8,128)}, u32[]{:S(2)}) copy-start(s32[64,6]{0,1:T(8,128)} %param.6) | copy-start | bytes 4612
  33.8 7.4 %collective-permute-start.13 = (f32[5,8,128]{2,1,0:T(8,128)S(1)}, f32[5,8,128]{2,1,0:T(8,128)S(1)}, u32[]{:S(2)}, u32[]{:S(2)}) collective-permute-start(f32[5,8,128]{2,1,0:T(8,128)S(1)} %get-tuple-element.58.refs_5_), channel_id=1, source_target_pairs={{0,2},{1,8},{2,0},{3,10},{4,6},{5,12},{6,4},{7,14},{8,1},{9,64},{1... | collective-permute-start | bytes 61448 | tf_op jit(solution)/shard_map/ppermute | solution.py:603
  34.0 7.2 %collective-permute-start.14 = (f32[5,8,128]{2,1,0:T(8,128)S(1)}, f32[5,8,128]{2,1,0:T(8,128)S(1)}, u32[]{:S(2)}, u32[]{:S(2)}) collective-permute-start(f32[5,8,128]{2,1,0:T(8,128)S(1)} %get-tuple-element.59.refs_6_), channel_id=1, source_target_pairs={{0,2},{1,3},{2,0},{3,1},{4,6},{5,7},{6,4},{7,5},{8,10},{9,11},{10,... | collective-permute-start | bytes 61448 | tf_op jit(solution)/shard_map/ppermute | solution.py:603
  34.6 6.6 %collective-permute-start.15 = (f32[5,8,128]{2,1,0:T(8,128)S(1)}, f32[5,8,128]{2,1,0:T(8,128)S(1)}, u32[]{:S(2)}, u32[]{:S(2)}) collective-permute-start(f32[5,8,128]{2,1,0:T(8,128)S(1)} %get-tuple-element.60.refs_7_), channel_id=1, source_target_pairs={{0,18},{1,19},{2,16},{3,17},{4,22},{5,23},{6,20},{7,21},{8,26},{9,... | collective-permute-start | bytes 61448 | tf_op jit(solution)/shard_map/ppermute | solution.py:603
  36.3 3.0 %copy-start.1 = (s32[64]{0:T(128)S(1)}, s32[64]{0:T(128)}, u32[]{:S(2)}) copy-start(s32[64]{0:T(128)} %param.7) | copy-start | bytes 772
  36.3 5.3 %collective-permute-start.16 = (f32[5,8,128]{2,1,0:T(8,128)S(1)}, f32[5,8,128]{2,1,0:T(8,128)S(1)}, u32[]{:S(2)}, u32[]{:S(2)}) collective-permute-start(f32[5,8,128]{2,1,0:T(8,128)S(1)} %get-tuple-element.61.refs_8_), channel_id=1, source_target_pairs={{0,4},{1,5},{2,6},{3,7},{4,0},{5,1},{6,2},{7,3},{8,12},{9,13},{10,... | collective-permute-start | bytes 61448 | tf_op jit(solution)/shard_map/ppermute | solution.py:603
  38.5 6.2 %collective-permute-start.17 = (f32[5,8,128]{2,1,0:T(8,128)S(1)}, f32[5,8,128]{2,1,0:T(8,128)S(1)}, u32[]{:S(2)}, u32[]{:S(2)}) collective-permute-start(f32[5,8,128]{2,1,0:T(8,128)S(1)} %get-tuple-element.62.refs_9_), channel_id=1, source_target_pairs={{0,1},{1,0},{2,3},{3,2},{4,32},{5,33},{6,34},{7,35},{8,9},{9,8},{1... | collective-permute-start | bytes 61448 | tf_op jit(solution)/shard_map/ppermute | solution.py:603
  45.4 8.2 %collective-permute-start.18 = (f32[11,4,512]{2,1,0:T(4,128)S(1)}, f32[11,4,512]{2,1,0:T(4,128)S(1)}, u32[]{:S(2)}, u32[]{:S(2)}) collective-permute-start(f32[11,4,512]{2,1,0:T(4,128)S(1)} %get-tuple-element.64), channel_id=1, source_target_pairs={{0,1},{1,2},{2,3},{3,4},{4,5},{5,6},{6,7},{7,8},{8,9},{9,10},{10,1... | collective-permute-start | bytes 270344 | tf_op jit(solution)/shard_map/ppermute | solution.py:670
